TPU v7x, 512 devices: a whole 4x8x8 slice. The times are simulated.
512 devices in a mesh: seq: 64 (over y_hi, z, core), tp: 8 (over x, y_lo).
Axes of the slice: x: 4, y: 8 (y_hi: 4, y_lo: 2; y = y_hi * 2 + y_lo), z: 8, core: 2. Of those that a mesh axis runs over, the one named last changes fastest.
Arguments:
- resid: bfloat16 [8192, 2048], P('seq'), may hold values from -1.5 to 1.5
- query: bfloat16 [8192, 1024], P('seq', 'tp'), may hold values from -6 to 6
- key_new: bfloat16 [8192, 1024], P('seq', 'tp'), may hold values from -6 to 6
- value_new: bfloat16 [8192, 1024], P('seq', 'tp'), may hold values from -6 to 6
- key_cache: bfloat16 [1024, 1024], P('seq', 'tp'), may hold values from -6 to 6
- value_cache: bfloat16 [1024, 1024], P('seq', 'tp'), may hold values from -6 to 6
- cache_len: int32 [64], replicated, may hold values from 0 to 16, as said below
- out_weight: bfloat16 [1024, 2048], P('tp'), may hold values from -0.1875 to 0.1875
- norm_gain: bfloat16 [2048], replicated, may hold values from 0.099609375 to 1.8984375
- router: bfloat16 [2048, 64], replicated, may hold values from -2 to 2
- expert_ids: int32 [8192, 6], P('seq'), may hold values from 0 to 63, all different within a row; in each aligned block of 128 rows (0 to 127, 128 to 255, ...) at most 18 rows name the same one
- w_gate: bfloat16 [64, 2048, 1408], P('seq', None, 'tp'), may hold values from -0.125 to 0.125
- w_up: bfloat16 [64, 2048, 1408], P('seq', None, 'tp'), may hold values from -0.125 to 0.125
- w_down: bfloat16 [64, 1408, 2048], P('seq', None, 'tp'), may hold values from -0.15625 to 0.15625
- w_shared_gate: bfloat16 [2048, 1408], P('seq', 'tp'), may hold values from -0.125 to 0.125
- w_shared_up: bfloat16 [2048, 1408], P('seq', 'tp'), may hold values from -0.125 to 0.125
- w_shared_down: bfloat16 [1408, 2048], P('tp', 'seq'), may hold values from -0.15625 to 0.15625
Outputs:
- mixed: bfloat16 [8192, 2048], P('seq', 'tp')
Inputs may be any that keep to these rules, and one draw needn't show every extreme that they name: `cache_len`: some cache block has all 16 rows valid and another has none. `expert_ids`: each row names 6 different experts; the rows of one device name no expert more than 18 times, a bound that some block reaches.
All inputs are finite; a program needn't handle non-finite values.
Results may differ from a plain program's by a relative error of at most 0.013.
Values may be sent and summed in bfloat16 or wider, within the bound.
No kernel may reach another device: no remote copies, remote signals or barrier semaphores. Data moves between devices by JAX's collectives and lax.ppermute only.
A program may use at most 64 MiB of HBM per device.

v0:
```python
import math

import jax
import jax.numpy as jnp
import numpy as np
from jax import lax
from jax.sharding import Mesh
from jax.sharding import PartitionSpec as P

D = 2048
HD = 128
TOPK = 6
CAP = 18

SEQ = ("yh", "z", "c")
TP = ("x", "yl")


def gather_seq(x):
    g = lax.all_gather(x, "yh", axis=0)
    g = lax.all_gather(g, "z", axis=0)
    g = lax.all_gather(g, "c", axis=0)
    return g


def tp_blocks(x, n_tp):
    out = [x]
    for k in range(1, n_tp):
        out.append(lax.ppermute(x, TP, [(j, (j + k) % n_tp) for j in range(n_tp)]))
    return out


def tp_gather(x, n_tp):
    b = jnp.broadcast_to(x[None], (n_tp,) + x.shape)
    return lax.all_to_all(b, TP, split_axis=0, concat_axis=0, tiled=True)


def local(
    resid,
    query,
    key_new,
    value_new,
    key_cache,
    value_cache,
    cache_len,
    out_weight,
    norm_gain,
    router,
    expert_ids,
    w_gate,
    w_up,
    w_down,
    w_shared_gate,
    w_shared_up,
    w_shared_down,
):
    tok_rows = query.shape[0]
    block_rows = key_cache.shape[0]
    n_yh, n_z, n_c = (lax.axis_size(a) for a in SEQ)
    n_x, n_yl = (lax.axis_size(a) for a in TP)
    n_seq = n_yh * n_z * n_c
    n_tp = n_x * n_yl
    seq_index = (lax.axis_index("yh") * n_z + lax.axis_index("z")) * n_c + lax.axis_index("c")
    tp_index = lax.axis_index("x") * n_yl + lax.axis_index("yl")
    width = D // n_tp

    wpack = jnp.stack([w_shared_gate, w_shared_up, w_shared_down.T], 0)
    w_rows = wpack.size // HD
    kv = jnp.concatenate(
        [key_cache, key_new, value_cache, value_new, wpack.reshape(w_rows, HD)], 0
    )
    g = lax.all_gather(kv, "yh", axis=0)
    g = lax.all_gather(g, "z", axis=0)
    other = lax.ppermute(g, "c", [(0, 1), (1, 0)])
    kvg = jnp.stack([g, other], 0).reshape(n_seq, kv.shape[0], HD)
    my_c = lax.axis_index("c")
    pos = jnp.arange(n_seq, dtype=jnp.int32)
    src = (pos % n_yh) * (n_z * n_c) + ((pos // n_yh) % n_z) * n_c + (pos // (n_yh * n_z) + my_c) % n_c
    s_ids = jnp.arange(n_seq, dtype=jnp.int32)
    pos_of_s = ((s_ids % n_c - my_c) % n_c) * (n_yh * n_z) + ((s_ids // n_c) % n_z) * n_yh + s_ids // (n_c * n_z)
    kv_rows = 2 * (block_rows + tok_rows)
    wg = jnp.take(kvg[:, kv_rows:], pos_of_s, axis=0).reshape(n_seq, 3, wpack.shape[1], wpack.shape[2])
    sg_w = wg[:, 0].reshape(n_seq * wpack.shape[1], wpack.shape[2])
    su_w = wg[:, 1].reshape(n_seq * wpack.shape[1], wpack.shape[2])
    sd_t = wg[:, 2].reshape(n_tp, n_seq // n_tp, wpack.shape[1], wpack.shape[2])
    ow_all = tp_gather(out_weight, n_tp)
    ck = kvg[:, :block_rows].reshape(n_seq * block_rows, HD)
    nk = kvg[:, block_rows:block_rows + tok_rows].reshape(n_seq * tok_rows, HD)
    cv = kvg[:, block_rows + tok_rows:2 * block_rows + tok_rows].reshape(n_seq * block_rows, HD)
    nv = kvg[:, 2 * block_rows + tok_rows:kv_rows].reshape(n_seq * tok_rows, HD)

    scale = 1.0 / math.sqrt(HD)
    s_c = jnp.dot(query, ck.T, preferred_element_type=jnp.float32) * scale
    s_n = jnp.dot(query, nk.T, preferred_element_type=jnp.float32) * scale
    c_open = (
        jnp.arange(block_rows, dtype=jnp.int32)[None, :] < cache_len[src][:, None]
    ).reshape(n_seq * block_rows)
    key_place = (src[:, None] * tok_rows + jnp.arange(tok_rows, dtype=jnp.int32)[None, :]).reshape(
        n_seq * tok_rows
    )
    query_place = seq_index * tok_rows + jnp.arange(tok_rows, dtype=jnp.int32)
    n_open = key_place[None, :] <= query_place[:, None]
    s_c = jnp.where(c_open[None, :], s_c, -jnp.inf)
    s_n = jnp.where(n_open, s_n, -jnp.inf)
    top = jnp.maximum(jnp.max(s_c, axis=-1, keepdims=True), jnp.max(s_n, axis=-1, keepdims=True))
    e_c = jnp.exp(s_c - top)
    e_n = jnp.exp(s_n - top)
    total = jnp.sum(e_c, axis=-1, keepdims=True) + jnp.sum(e_n, axis=-1, keepdims=True)
    p_c = (e_c / total).astype(jnp.bfloat16)
    p_n = (e_n / total).astype(jnp.bfloat16)
    attn = jnp.dot(p_c, cv, preferred_element_type=jnp.float32) + jnp.dot(
        p_n, nv, preferred_element_type=jnp.float32
    )
    attn = attn.astype(jnp.bfloat16)

    sd_rows = sd_t[0].size // HD
    mixed_in = jnp.concatenate(
        [jnp.broadcast_to(attn[None], (n_tp,) + attn.shape), sd_t.reshape(n_tp, sd_rows, HD)], 1
    )
    mixed_out = lax.all_to_all(mixed_in, TP, split_axis=0, concat_axis=0, tiled=True)
    attn_all = mixed_out[:, :tok_rows]
    sd_own = mixed_out[:, tok_rows:].reshape(sd_t.shape)
    projected = jnp.einsum("tqd,tdn->qn", attn_all, ow_all, preferred_element_type=jnp.float32)
    hidden_state = resid.astype(jnp.float32) + projected
    mean_square = jnp.mean(hidden_state * hidden_state, axis=-1, keepdims=True)
    normed = (hidden_state * lax.rsqrt(mean_square + 1e-06) * norm_gain.astype(jnp.float32)).astype(
        jnp.bfloat16
    )
    own_hidden = lax.dynamic_slice_in_dim(hidden_state, tp_index * width, width, 1)
    own_normed = lax.dynamic_slice_in_dim(normed, tp_index * width, width, 1)

    logits = jnp.dot(normed, router, preferred_element_type=jnp.float32)
    expert_count = router.shape[1]
    expert_range = jnp.arange(expert_count, dtype=jnp.int32)
    picked = jnp.sum(
        jnp.where(expert_ids[:, :, None] == expert_range[None, None, :], logits[:, None, :], 0.0),
        axis=-1,
    )
    gates = jax.nn.softmax(picked, axis=-1)

    shared_gate = jnp.dot(normed, sg_w, preferred_element_type=jnp.float32)
    shared_up = jnp.dot(normed, su_w, preferred_element_type=jnp.float32)
    shared_inner = (jax.nn.silu(shared_gate) * shared_up).astype(jnp.bfloat16)

    flat_ids = expert_ids.reshape(tok_rows * TOPK)
    one_hot = (flat_ids[:, None] == expert_range[None, :]).astype(jnp.int32)
    before = jnp.cumsum(one_hot, axis=0) - one_hot
    slot = jnp.sum(one_hot * before, axis=1)
    dest = flat_ids * CAP + slot
    slots = expert_count * CAP
    place = (dest[None, :] == jnp.arange(slots, dtype=jnp.int32)[:, None]).reshape(
        slots, tok_rows, TOPK
    )
    dispatch = jnp.any(place, axis=-1).astype(jnp.bfloat16)
    buffer = jnp.dot(dispatch, own_normed, preferred_element_type=jnp.float32).astype(jnp.bfloat16)
    buffer = buffer.reshape(expert_count, CAP, width)
    recv = lax.all_to_all(buffer, SEQ, split_axis=0, concat_axis=0, tiled=True)
    ff = w_gate.shape[2]
    rows_flat = recv.reshape(slots, width)
    inner_rows = shared_inner.size // width
    carried = jnp.concatenate([rows_flat, shared_inner.reshape(inner_rows, width)], 0)
    wg_b = w_gate[0].reshape(n_tp, width, ff)
    wu_b = w_up[0].reshape(n_tp, width, ff)
    wd_b = w_down[0].reshape(n_tp, ff, w_down.shape[2])
    both = tp_gather(carried, n_tp)
    rows_all = both[:, :slots]
    sinner_all = both[:, slots:].reshape((n_tp,) + shared_inner.shape)
    shared_own = jnp.einsum("tqf,tsjf->qsj", sinner_all, sd_own, preferred_element_type=jnp.float32)
    gate_pre = jnp.einsum("tsc,tcf->sf", rows_all, wg_b, preferred_element_type=jnp.float32)
    up_pre = jnp.einsum("tsc,tcf->sf", rows_all, wu_b, preferred_element_type=jnp.float32)
    inner = (jax.nn.silu(gate_pre) * up_pre).astype(jnp.bfloat16)
    inner_all = tp_gather(inner, n_tp)
    out = jnp.einsum("tsf,tfn->sn", inner_all, wd_b, preferred_element_type=jnp.float32)
    out = out.astype(jnp.bfloat16).reshape(expert_count, CAP, w_down.shape[2])
    shared_own = shared_own.reshape(tok_rows, width)
    returned = lax.all_to_all(out, SEQ, split_axis=0, concat_axis=0, tiled=True)
    picked_rows = returned.reshape(slots, width)[dest]
    weighted = picked_rows.astype(jnp.float32) * gates.reshape(tok_rows * TOPK)[:, None]
    routed = jnp.sum(weighted.reshape(tok_rows, TOPK, width), axis=1)
    return (own_hidden + shared_own + routed).astype(jnp.bfloat16)


def solution(mesh):
    n_seq, n_tp = mesh.devices.shape
    fine = Mesh(mesh.devices.reshape(n_seq // 16, 8, 2, n_tp // 2, 2), SEQ + TP)
    return jax.shard_map(
        local,
        mesh=fine,
        in_specs=(
            P(SEQ, None),
            P(SEQ, TP),
            P(SEQ, TP),
            P(SEQ, TP),
            P(SEQ, TP),
            P(SEQ, TP),
            P(),
            P(TP, None),
            P(),
            P(),
            P(SEQ, None),
            P(SEQ, None, TP),
            P(SEQ, None, TP),
            P(SEQ, None, TP),
            P(SEQ, TP),
            P(SEQ, TP),
            P(TP, SEQ),
        ),
        out_specs=P(SEQ, TP),
        check_vma=False,
    )
```

profile of v0, /device:TPU:1, one launch (start us, length us, event | category | flops | bytes accessed | tf_op | source)
XLA Modules:
  0.0 386.5 jit_solution(3856518325411960046)
XLA Ops:
  10.4 17.2 %all-gather.2 = bf16[4,420,128]{2,1,0:T(8,128)(2,1)} all-gather(bf16[1,420,128]{2,1,0:T(8,128)(2,1)S(1)} %bitcast.121), channel_id=2, replica_groups=mesh['yh'=4,'z'=8,'c'=2,'x'=4,'yl'=2] {'yh'}, dimensions={0}, use_global_device_ids=true | all-gather | bytes 537600 | tf_op jit(solution)/shard_map/all_gather | solution.py:72
  27.6 56.6 %all-gather.5.cloned.1.call-done = bf16[32,420,128]{2,1,0:T(8,128)(2,1)} async-done(((bf16[4,420,128]{2,1,0:T(8,128)(2,1)}), bf16[32,420,128]{2,1,0:T(8,128)(2,1)}) %all-gather.5.cloned.1.call-update) | async-done | bytes 3440656 | tf_op jit(solution)/shard_map/all_gather | solution.py:73
  84.3 5.1 %copy.63 = bf16[8,4,420,128]{3,0,2,1:T(8,128)(2,1)} copy(bf16[8,4,420,128]{3,2,1,0:T(8,128)(2,1)} %bitcast.108) | data formatting | bytes 6881280 | tf_op jit(solution)/shard_map/all_gather | solution.py:73
  89.4 2.7 collective-permute-start
  92.1 2.6 broadcast_in_dim.52
  94.7 5.0 %all-to-all-start.1 = ((bf16[8,128,2048]{2,1,0:T(8,128)(2,1)}), bf16[8,128,2048]{2,1,0:T(8,128)(2,1)}, u32[]{:S(2)}, u32[]{:S(2)}) async-start(bf16[8,128,2048]{2,1,0:T(8,128)(2,1)} %broadcast_in_dim.52), calls=%async_computation.1 | async-start | bytes 8388608 | tf_op jit(solution)/shard_map/all_to_all | solution.py:35
  100.9 3.3 copy.64
  104.2 2.6 pad_maximum_fusion
  107.8 2.8 copy-done.2
  110.6 1.5 slice.66
  112.1 2.6 gather_fusion.1
  114.7 5.9 %gather.14 = bf16[64,3,32,176]{3,2,1,0:T(8,128)(2,1)} reshape(bf16[64,132,128]{2,1,0:T(8,128)(2,1)S(1)} %gather_fusion.1) | data formatting | bytes 4325376 | tf_op jit(solution)/shard_map/jit(_take)/gather | solution.py:82
  120.6 2.2 broadcast_select_fusion
  122.8 1.6 fusion.78
  124.5 1.5 reshape_reshape_squeeze.3
  127.4 2.7 fusion.77
  130.1 1.3 fusion.80
  131.6 1.1 fusion.6
  135.1 14.1 %all-to-all-done.1 = bf16[8,128,2048]{2,1,0:T(8,128)(2,1)} async-done(((bf16[8,128,2048]{2,1,0:T(8,128)(2,1)}), bf16[8,128,2048]{2,1,0:T(8,128)(2,1)}, u32[]{:S(2)}, u32[]{:S(2)}) %all-to-all-start.1) | async-done | bytes 4194336 | tf_op jit(solution)/shard_map/all_to_all | solution.py:35
  149.1 3.8 all-to-all-start
  153.4 1.8 reduce-window.6
  157.1 9.2 %all-to-all-done = bf16[8,480,128]{2,1,0:T(8,128)(2,1)S(1)} async-done(((bf16[8,480,128]{2,1,0:T(8,128)(2,1)}), bf16[8,480,128]{2,1,0:T(8,128)(2,1)S(1)}, u32[]{:S(2)}, u32[]{:S(2)}) %all-to-all-start) | async-done | bytes 983072 | tf_op jit(solution)/shard_map/all_to_all | solution.py:120
  166.3 3.1 multiply_reduce_fusion.1
  169.6 1.1 convolution_convert_fusion
  170.7 2.1 reshape.528
  172.8 11.9 %all-to-all-start.2 = ((bf16[64,18,256]{2,1,0:T(8,128)(2,1)}), bf16[64,18,256]{2,1,0:T(8,128)(2,1)}, u32[]{:S(2)}, u32[]{:S(2)}) async-start(bf16[64,18,256]{2,1,0:T(8,128)(2,1)} %reshape.528), calls=%async_computation.2 | async-start | bytes 1572864 | tf_op jit(solution)/shard_map/all_to_all | solution.py:157
  184.7 1.7 fusion.81
  186.5 1.7 fusion.27
  188.5 20.5 %all-to-all-done.2 = bf16[64,18,256]{2,1,0:T(8,128)(2,1)} async-done(((bf16[64,18,256]{2,1,0:T(8,128)(2,1)}), bf16[64,18,256]{2,1,0:T(8,128)(2,1)}, u32[]{:S(2)}, u32[]{:S(2)}) %all-to-all-start.2) | async-done | bytes 589856 | tf_op jit(solution)/shard_map/all_to_all | solution.py:157
  208.9 2.1 reshape.529
  211.0 1.1 pad_maximum_fusion.2
  212.1 2.6 broadcast_in_dim.53
  214.7 9.4 %all-to-all-start.3 = ((bf16[8,1240,256]{2,1,0:T(8,128)(2,1)}), bf16[8,1240,256]{2,1,0:T(8,128)(2,1)}, u32[]{:S(2)}, u32[]{:S(2)}) async-start(bf16[8,1240,256]{2,1,0:T(8,128)(2,1)} %broadcast_in_dim.53), calls=%async_computation.3 | async-start | bytes 10158080 | tf_op jit(solution)/shard_map/all_to_all | solution.py:35
  224.1 2.2 copy.81
  226.3 2.2 copy.82
  228.5 54.4 %all-to-all-done.3 = bf16[8,1240,256]{2,1,0:T(8,128)(2,1)} async-done(((bf16[8,1240,256]{2,1,0:T(8,128)(2,1)}), bf16[8,1240,256]{2,1,0:T(8,128)(2,1)}, u32[]{:S(2)}, u32[]{:S(2)}) %all-to-all-start.3) | async-done | bytes 5079072 | tf_op jit(solution)/shard_map/all_to_all | solution.py:35
  282.9 4.3 %fusion.9 = f32[1152,176]{0,1:T(8,128)S(1)} fusion(bf16[8,1240,256]{2,1,0:T(8,128)(2,1)} %all-to-all-done.3, bf16[8,256,176]{1,0,2:T(8,128)(2,1)} %bitcast.119), kind=kOutput, calls=%fused_computation.20 | convolution fusion | flops 830472192 | bytes 6250496 | tf_op jit(solution)/shard_map/tsc,tcf->sf/dot_general | solution.py:169
  287.2 4.0 %fusion.18 = bf16[1152,176]{0,1:T(8,128)(2,1)S(1)} fusion(bf16[8,1240,256]{2,1,0:T(8,128)(2,1)} %all-to-all-done.3, f32[1152,176]{0,1:T(8,128)S(1)} %fusion.9, bf16[8,256,176]{1,0,2:T(8,128)(2,1)S(1)} %bitcast.118), kind=kOutput, calls=%fused_computation.23 | convolution fusion | flops 831688704 | bytes 6656000 | tf_op jit(solution)/shard_map/tsc,tcf->sf/dot_general | solution.py:170
  291.4 41.1 %all_to_all.30 = bf16[8,1152,176]{1,2,0:T(8,128)(2,1)S(1)} all-to-all(bf16[8,1152,176]{1,2,0:T(8,128)(2,1)S(1)} %broadcast_in_dim.54), channel_id=1, replica_groups=mesh['yh'=4,'z'=8,'c'=2,'x'=4,'yl'=2] {'x','yl'}, dimensions={0} | all-to-all | bytes 6488064 | tf_op jit(solution)/shard_map/all_to_all | solution.py:35
  332.6 2.0 fusion.8
  334.5 2.1 reshape.533
  336.6 11.4 %all-to-all-start.5 = ((bf16[64,18,256]{2,1,0:T(8,128)(2,1)}), bf16[64,18,256]{2,1,0:T(8,128)(2,1)}, u32[]{:S(2)}, u32[]{:S(2)}) async-start(bf16[64,18,256]{2,1,0:T(8,128)(2,1)} %reshape.533), calls=%async_computation.5 | async-start | bytes 1572864 | tf_op jit(solution)/shard_map/all_to_all | solution.py:176
  350.5 3.5 reshape.532
  355.0 1.9 reshape.531
  356.9 15.8 %all-to-all-done.5 = bf16[64,18,256]{2,1,0:T(8,128)(2,1)} async-done(((bf16[64,18,256]{2,1,0:T(8,128)(2,1)}), bf16[64,18,256]{2,1,0:T(8,128)(2,1)}, u32[]{:S(2)}, u32[]{:S(2)}) %all-to-all-start.5) | async-done | bytes 589856 | tf_op jit(solution)/shard_map/all_to_all | solution.py:176
  372.7 1.3 reshape.534
  374.0 2.7 gather_fusion.2
  377.2 2.5 fusion.26
  (77 shorter events, 16.8 us)
Async XLA Ops:
  6.5 326.0 %copy-start = (bf16[1,1408,256]{2,1,0:T(8,128)(2,1)S(1)}, bf16[1,1408,256]{2,1,0:T(8,128)(2,1)}, u32[]{:S(2)}) copy-start(bf16[1,1408,256]{2,1,0:T(8,128)(2,1)} %param.30) | copy-start | bytes 2162692
  6.5 77.7 %all-gather.5.cloned.1.call-start = ((), (), s32[]{:S(2)}) async-start(), calls=%async_computation.6 | async-start | bytes 3907584 | tf_op jit(solution)/shard_map/all_gather | solution.py:73
  27.6 64.5 %copy-start.4 = (bf16[128,2048]{1,0:T(8,128)(2,1)S(1)}, bf16[128,2048]{1,0:T(8,128)(2,1)}, u32[]{:S(2)}) copy-start(bf16[128,2048]{1,0:T(8,128)(2,1)} %param.24) | copy-start | bytes 1572868
  89.4 14.9 %collective-permute-start = (bf16[8,4,420,128]{3,0,2,1:T(8,128)(2,1)}, bf16[8,4,420,128]{3,0,2,1:T(8,128)(2,1)}, u32[]{:S(2)}, u32[]{:S(2)}) collective-permute-start(bf16[8,4,420,128]{3,0,2,1:T(8,128)(2,1)} %copy.63), channel_id=1, source_target_pairs={{0,8},{8,0},{1,9},{9,1},{2,10},{10,2},{3,11},{11,3},{4,12},{12,4},... | collective-permute-start | bytes 10321928 | tf_op jit(solution)/shard_map/ppermute | solution.py:74
  94.7 5.1 %copy-start.1 = (s32[64]{0:T(128)S(1)}, s32[64]{0:T(128)}, u32[]{:S(2)}) copy-start(s32[64]{0:T(128)} %param.23) | copy-start | bytes 772
  94.7 54.4 %all-to-all-start.1 = ((bf16[8,128,2048]{2,1,0:T(8,128)(2,1)}), bf16[8,128,2048]{2,1,0:T(8,128)(2,1)}, u32[]{:S(2)}, u32[]{:S(2)}) async-start(bf16[8,128,2048]{2,1,0:T(8,128)(2,1)} %broadcast_in_dim.52), calls=%async_computation.1 | async-start | bytes 8388608 | tf_op jit(solution)/shard_map/all_to_all | solution.py:35
  107.8 2.8 copy-start.2
  122.8 4.2 %copy-start.6 = (bf16[128,128]{1,0:T(8,128)(2,1)S(1)}, bf16[128,128]{1,0:T(8,128)(2,1)}, u32[]{:S(2)}) copy-start(bf16[128,128]{1,0:T(8,128)(2,1)} %param.18) | copy-start | bytes 98308
  133.7 19.2 %copy-start.7 = (s32[128,6]{0,1:T(8,128)S(1)}, s32[128,6]{0,1:T(8,128)}, u32[]{:S(2)}) copy-start(s32[128,6]{0,1:T(8,128)} %param.27) | copy-start | bytes 9220
  133.7 19.6 %copy-start.8 = (bf16[2048]{0:T(1024)(128)(2,1)S(1)}, bf16[2048]{0:T(1024)(128)(2,1)}, u32[]{:S(2)}) copy-start(bf16[2048]{0:T(1024)(128)(2,1)} %param.25) | copy-start | bytes 12292
  149.1 17.1 %all-to-all-start = ((bf16[8,480,128]{2,1,0:T(8,128)(2,1)}), bf16[8,480,128]{2,1,0:T(8,128)(2,1)S(1)}, u32[]{:S(2)}, u32[]{:S(2)}) async-start(bf16[8,480,128]{2,1,0:T(8,128)(2,1)} %pad_maximum_fusion.1), calls=%async_computation | async-start | bytes 1966080 | tf_op jit(solution)/shard_map/all_to_all | solution.py:120
  172.8 36.1 %all-to-all-start.2 = ((bf16[64,18,256]{2,1,0:T(8,128)(2,1)}), bf16[64,18,256]{2,1,0:T(8,128)(2,1)}, u32[]{:S(2)}, u32[]{:S(2)}) async-start(bf16[64,18,256]{2,1,0:T(8,128)(2,1)} %reshape.528), calls=%async_computation.2 | async-start | bytes 1572864 | tf_op jit(solution)/shard_map/all_to_all | solution.py:157
  214.7 68.2 %all-to-all-start.3 = ((bf16[8,1240,256]{2,1,0:T(8,128)(2,1)}), bf16[8,1240,256]{2,1,0:T(8,128)(2,1)}, u32[]{:S(2)}, u32[]{:S(2)}) async-start(bf16[8,1240,256]{2,1,0:T(8,128)(2,1)} %broadcast_in_dim.53), calls=%async_computation.3 | async-start | bytes 10158080 | tf_op jit(solution)/shard_map/all_to_all | solution.py:35
  282.9 4.3 %copy-start.3 = (bf16[22,8,8,256]{3,2,1,0:T(8,128)(2,1)S(1)}, bf16[22,8,8,256]{3,2,1,0:T(8,128)(2,1)}, u32[]{:S(2)}) copy-start(bf16[22,8,8,256]{3,2,1,0:T(8,128)(2,1)} %copy.82) | copy-start | bytes 2162692
  332.6 16.5 %copy-start.5 = (bf16[2048,64]{0,1:T(8,128)(2,1)S(1)}, bf16[2048,64]{0,1:T(8,128)(2,1)}, u32[]{:S(2)}) copy-start(bf16[2048,64]{0,1:T(8,128)(2,1)} %param.26) | copy-start | bytes 786436
  336.6 36.1 %all-to-all-start.5 = ((bf16[64,18,256]{2,1,0:T(8,128)(2,1)}), bf16[64,18,256]{2,1,0:T(8,128)(2,1)}, u32[]{:S(2)}, u32[]{:S(2)}) async-start(bf16[64,18,256]{2,1,0:T(8,128)(2,1)} %reshape.533), calls=%async_computation.5 | async-start | bytes 1572864 | tf_op jit(solution)/shard_map/all_to_all | solution.py:176
Sparse Core Ops, SparseCore 0:
  27.7 56.4 all-gather.4
where the time goes:
time: 388 us; the launch traced here: 387 us
  waiting for transfers between devices  171 us (44%)
  local copies, waits for them, and re-layouts  62.7 us (16%)
  blocking collectives  58.3 us (15%)
  starting transfers between devices  44.3 us (11%)
  matrix products  23.7 us (6%)
  between operations  13.8 us (4%)
  other arithmetic  13.1 us (3%)
    all_to_all x2, waiting for transfers between devices, tp_gather(): return lax.all_to_all(b, TP, split_axis=0, concat_axis=0, tiled=True)  68.5 us
    all_gather x1, waiting for transfers between devices, local(): g = lax.all_gather(g, 'z', axis=0)  56.6 us
    all_to_all x1, blocking collectives, tp_gather(): return lax.all_to_all(b, TP, split_axis=0, concat_axis=0, tiled=True)  41.1 us
    all_to_all x1, waiting for transfers between devices, local(): recv = lax.all_to_all(buffer, SEQ, split_axis=0, concat_axis=0, tiled=True)  20.5 us
    all_gather x1, blocking collectives, local(): g = lax.all_gather(kv, 'yh', axis=0)  17.2 us
    all_to_all x1, waiting for transfers between devices, local(): returned = lax.all_to_all(out, SEQ, split_axis=0, concat_axis=0, tiled=True)  15.8 us
    all_to_all x2, starting transfers between devices, tp_gather(): return lax.all_to_all(b, TP, split_axis=0, concat_axis=0, tiled=True)  14.5 us
    all_to_all x1, starting transfers between devices, local(): recv = lax.all_to_all(buffer, SEQ, split_axis=0, concat_axis=0, tiled=True)  11.9 us
  transfers between devices with their start and end apart: 7, of which 6 were waited for; matrix products, arithmetic and copies ran while one was open for 14% of the time, Pallas kernels for 0%

commit v1 on v0

--- a/solution.py
+++ b/solution.py
@@ -64,30 +64,35 @@
     tp_index = lax.axis_index("x") * n_yl + lax.axis_index("yl")
     width = D // n_tp
 
-    wpack = jnp.stack([w_shared_gate, w_shared_up, w_shared_down.T], 0)
-    w_rows = wpack.size // HD
-    kv = jnp.concatenate(
-        [key_cache, key_new, value_cache, value_new, wpack.reshape(w_rows, HD)], 0
-    )
-    g = lax.all_gather(kv, "yh", axis=0)
-    g = lax.all_gather(g, "z", axis=0)
+    kv = jnp.concatenate([key_cache, key_new, value_cache, value_new], 0)
+    g = lax.all_gather(kv, ("yh", "z"), axis=0)
     other = lax.ppermute(g, "c", [(0, 1), (1, 0)])
     kvg = jnp.stack([g, other], 0).reshape(n_seq, kv.shape[0], HD)
     my_c = lax.axis_index("c")
     pos = jnp.arange(n_seq, dtype=jnp.int32)
-    src = (pos % n_yh) * (n_z * n_c) + ((pos // n_yh) % n_z) * n_c + (pos // (n_yh * n_z) + my_c) % n_c
+    src = ((pos % (n_yh * n_z)) // n_z) * (n_z * n_c) + (pos % n_z) * n_c + (
+        pos // (n_yh * n_z) + my_c
+    ) % n_c
     s_ids = jnp.arange(n_seq, dtype=jnp.int32)
-    pos_of_s = ((s_ids % n_c - my_c) % n_c) * (n_yh * n_z) + ((s_ids // n_c) % n_z) * n_yh + s_ids // (n_c * n_z)
-    kv_rows = 2 * (block_rows + tok_rows)
-    wg = jnp.take(kvg[:, kv_rows:], pos_of_s, axis=0).reshape(n_seq, 3, wpack.shape[1], wpack.shape[2])
+    pos_of_s = ((s_ids % n_c - my_c) % n_c) * (n_yh * n_z) + (s_ids // (n_c * n_z)) * n_z + (
+        s_ids // n_c
+    ) % n_z
+    ck = kvg[:, :block_rows].reshape(n_seq * block_rows, HD)
+    nk = kvg[:, block_rows:block_rows + tok_rows].reshape(n_seq * tok_rows, HD)
+    cv = kvg[:, block_rows + tok_rows:2 * block_rows + tok_rows].reshape(n_seq * block_rows, HD)
+    nv = kvg[:, 2 * block_rows + tok_rows:].reshape(n_seq * tok_rows, HD)
+
+    wpack = jnp.stack([w_shared_gate, w_shared_up, w_shared_down.T], 0)
+    w_rows = wpack.size // HD
+    wflat = wpack.reshape(w_rows, HD) + (g[0, :1, :] * 0).astype(wpack.dtype)
+    wgath = lax.all_gather(wflat, ("yh", "z"), axis=0)
+    wother = lax.ppermute(wgath, "c", [(0, 1), (1, 0)])
+    wk = jnp.stack([wgath, wother], 0).reshape(n_seq, w_rows, HD)
+    wg = jnp.take(wk, pos_of_s, axis=0).reshape(n_seq, 3, wpack.shape[1], wpack.shape[2])
     sg_w = wg[:, 0].reshape(n_seq * wpack.shape[1], wpack.shape[2])
     su_w = wg[:, 1].reshape(n_seq * wpack.shape[1], wpack.shape[2])
     sd_t = wg[:, 2].reshape(n_tp, n_seq // n_tp, wpack.shape[1], wpack.shape[2])
     ow_all = tp_gather(out_weight, n_tp)
-    ck = kvg[:, :block_rows].reshape(n_seq * block_rows, HD)
-    nk = kvg[:, block_rows:block_rows + tok_rows].reshape(n_seq * tok_rows, HD)
-    cv = kvg[:, block_rows + tok_rows:2 * block_rows + tok_rows].reshape(n_seq * block_rows, HD)
-    nv = kvg[:, 2 * block_rows + tok_rows:kv_rows].reshape(n_seq * tok_rows, HD)
 
     scale = 1.0 / math.sqrt(HD)
     s_c = jnp.dot(query, ck.T, preferred_element_type=jnp.float32) * scale

time: 388 us -> 456 us (1.18)
  waiting for transfers between devices: 171 us -> 259 us
  blocking collectives: 58.3 us -> 41.1 us
  local copies, waits for them, and re-layouts: 62.7 us -> 47.4 us
  starting transfers between devices: 44.3 us -> 54.4 us
    all_gather x1 -> x2, waiting for transfers between devices: 56.6 us -> 158 us  [the longest x1 83.2 us: local(): g = lax.all_gather(kv, ('yh', 'z'), axis=0)]
    all_gather x1 -> x0, blocking collectives: 17.2 us -> none  [local(): g = lax.all_gather(kv, 'yh', axis=0)]
    all_to_all x2, waiting for transfers between devices: 68.5 us -> 54.4 us  [tp_gather(): return lax.all_to_all(b, TP, split_axis=0, concat_axis=0, tiled=True)]
    ppermute x0 -> x1, starting transfers between devices: none -> 8.05 us  [local(): wother = lax.ppermute(wgath, 'c', [(0, 1), (1, 0)])]
    unnamed x25 -> x27, local copies, waits for them, and re-layouts: 10.3 us -> 5.01 us
  transfers between devices with their start and end apart: 7 -> 9, of which waited for: 6 -> 6; matrix products, arithmetic and copies ran while one was open for 14% -> 11% of each run, Pallas kernels for 0% -> 0%
where the time goes in v1:
time: 456 us; the launch traced here: 454 us
  waiting for transfers between devices  259 us (57%)
  starting transfers between devices  54.4 us (12%)
  local copies, waits for them, and re-layouts  47.4 us (10%)
  blocking collectives  41.1 us (9%)
  matrix products  23.7 us (5%)
  other arithmetic  14.9 us (3%)
  between operations  13.9 us (3%)
    all_gather x1, waiting for transfers between devices, local(): g = lax.all_gather(kv, ('yh', 'z'), axis=0)  83.2 us
    all_gather x1, waiting for transfers between devices, local(): wgath = lax.all_gather(wflat, ('yh', 'z'), axis=0)  74.4 us
    all_to_all x2, waiting for transfers between devices, tp_gather(): return lax.all_to_all(b, TP, split_axis=0, concat_axis=0, tiled=True)  54.4 us
    all_to_all x1, blocking collectives, tp_gather(): return lax.all_to_all(b, TP, split_axis=0, concat_axis=0, tiled=True)  41.1 us
    all_to_all x1, waiting for transfers between devices, local(): recv = lax.all_to_all(buffer, SEQ, split_axis=0, concat_axis=0, tiled=True)  20.4 us
    all_to_all x1, waiting for transfers between devices, local(): returned = lax.all_to_all(out, SEQ, split_axis=0, concat_axis=0, tiled=True)  15.8 us
    all_to_all x2, starting transfers between devices, tp_gather(): return lax.all_to_all(b, TP, split_axis=0, concat_axis=0, tiled=True)  15.4 us
    all_to_all x1, starting transfers between devices, local(): returned = lax.all_to_all(out, SEQ, split_axis=0, concat_axis=0, tiled=True)  11.4 us
  transfers between devices with their start and end apart: 9, of which 6 were waited for; matrix products, arithmetic and copies ran while one was open for 11% of the time, Pallas kernels for 0%

profile of v1, /device:TPU:1, one launch (start us, length us, event | category | flops | bytes accessed | tf_op | source)
XLA Modules:
  0.0 454.4 jit_solution(14796791556568755014)
XLA Ops:
  6.5 1.5 pad_maximum_fusion.4
  8.1 3.5 broadcast_in_dim.52
  11.6 6.0 %all-to-all-start.1 = ((bf16[8,128,2048]{2,1,0:T(8,128)(2,1)}), bf16[8,128,2048]{2,1,0:T(8,128)(2,1)}, u32[]{:S(2)}, u32[]{:S(2)}) async-start(bf16[8,128,2048]{2,1,0:T(8,128)(2,1)} %broadcast_in_dim.52), calls=%async_computation.1 | async-start | bytes 8388608 | tf_op jit(solution)/shard_map/all_to_all | solution.py:35
  17.8 83.2 %all-gather.6.cloned.1.call-done = bf16[9216,128]{1,0:T(8,128)(2,1)} async-done(((bf16[288,128]{1,0:T(8,128)(2,1)}), bf16[9216,128]{1,0:T(8,128)(2,1)}) %all-gather.6.cloned.1.call-update) | async-done | bytes 2359312 | tf_op jit(solution)/shard_map/all_gather | solution.py:68
  101.0 6.2 %collective-permute-start = (bf16[32,288,128]{2,1,0:T(8,128)(2,1)}, bf16[32,288,128]{2,1,0:T(8,128)(2,1)}, u32[]{:S(2)}, u32[]{:S(2)}) collective-permute-start(bf16[32,288,128]{2,1,0:T(8,128)(2,1)} %bitcast.119), channel_id=1, source_target_pairs={{0,8},{8,0},{1,9},{9,1},{2,10},{10,2},{3,11},{11,3},{4,12},{12,4},... | collective-permute-start | bytes 7077896 | tf_op jit(solution)/shard_map/ppermute | solution.py:69
  109.7 74.4 %all-gather.4.cloned.1.call-done = bf16[32,132,128]{2,1,0:T(8,128)(2,1)} async-done(((bf16[1,132,128]{2,1,0:T(8,128)(2,1)}), bf16[32,132,128]{2,1,0:T(8,128)(2,1)}) %all-gather.4.cloned.1.call-update) | async-done | bytes 1081360 | tf_op jit(solution)/shard_map/all_gather | solution.py:88
  184.1 1.4 copy.48
  185.5 8.1 %collective-permute-start.1 = (bf16[32,132,128]{2,0,1:T(8,128)(2,1)S(1)}, bf16[32,132,128]{2,0,1:T(8,128)(2,1)S(1)}, u32[]{:S(2)}, u32[]{:S(2)}) collective-permute-start(bf16[32,132,128]{2,0,1:T(8,128)(2,1)S(1)} %copy.48), channel_id=1, source_target_pairs={{0,8},{8,0},{1,9},{9,1},{2,10},{10,2},{3,11},{11,3},{4,12},{12,4},... | collective-permute-start | bytes 3244040 | tf_op jit(solution)/shard_map/ppermute | solution.py:89
  193.6 2.1 pad_maximum_fusion
  196.6 1.3 fusion.77
  197.9 1.1 fusion.6
  199.2 1.0 fusion.22
  201.7 2.3 gather_fusion.1
  204.0 7.4 %gather.14 = bf16[64,3,32,176]{3,2,1,0:T(8,128)(2,1)} reshape(bf16[64,132,128]{2,1,0:T(8,128)(2,1)} %gather_fusion.1) | data formatting | bytes 4325376 | tf_op jit(solution)/shard_map/jit(_take)/gather | solution.py:91
  211.4 2.2 broadcast_select_fusion
  213.6 1.7 fusion.75
  215.4 1.5 reshape_reshape_squeeze.3
  216.9 1.0 pad_maximum_fusion.2
  217.9 4.1 all-to-all-start
  222.4 1.8 reduce-window.6
  226.1 10.7 %all-to-all-done = bf16[8,480,128]{2,1,0:T(8,128)(2,1)S(1)} async-done(((bf16[8,480,128]{2,1,0:T(8,128)(2,1)}), bf16[8,480,128]{2,1,0:T(8,128)(2,1)S(1)}, u32[]{:S(2)}, u32[]{:S(2)}) %all-to-all-start) | async-done | bytes 983072 | tf_op jit(solution)/shard_map/all_to_all | solution.py:125
  236.8 3.1 multiply_reduce_fusion.1
  240.1 1.1 convolution_convert_fusion
  241.3 2.1 reshape.581
  243.4 9.2 %all-to-all-start.2 = ((bf16[64,18,256]{2,1,0:T(8,128)(2,1)}), bf16[64,18,256]{2,1,0:T(8,128)(2,1)}, u32[]{:S(2)}, u32[]{:S(2)}) async-start(bf16[64,18,256]{2,1,0:T(8,128)(2,1)} %reshape.581), calls=%async_computation.2 | async-start | bytes 1572864 | tf_op jit(solution)/shard_map/all_to_all | solution.py:162
  252.6 1.7 fusion.78
  254.3 1.7 fusion.27
  256.3 20.4 %all-to-all-done.2 = bf16[64,18,256]{2,1,0:T(8,128)(2,1)} async-done(((bf16[64,18,256]{2,1,0:T(8,128)(2,1)}), bf16[64,18,256]{2,1,0:T(8,128)(2,1)}, u32[]{:S(2)}, u32[]{:S(2)}) %all-to-all-start.2) | async-done | bytes 589856 | tf_op jit(solution)/shard_map/all_to_all | solution.py:162
  276.7 2.1 reshape.582
  278.8 1.1 pad_maximum_fusion.3
  279.9 2.6 broadcast_in_dim.53
  282.5 9.4 %all-to-all-start.3 = ((bf16[8,1240,256]{2,1,0:T(8,128)(2,1)}), bf16[8,1240,256]{2,1,0:T(8,128)(2,1)}, u32[]{:S(2)}, u32[]{:S(2)}) async-start(bf16[8,1240,256]{2,1,0:T(8,128)(2,1)} %broadcast_in_dim.53), calls=%async_computation.3 | async-start | bytes 10158080 | tf_op jit(solution)/shard_map/all_to_all | solution.py:35
  291.9 2.2 copy.65
  294.1 2.2 copy.66
  296.2 54.4 %all-to-all-done.3 = bf16[8,1240,256]{2,1,0:T(8,128)(2,1)} async-done(((bf16[8,1240,256]{2,1,0:T(8,128)(2,1)}), bf16[8,1240,256]{2,1,0:T(8,128)(2,1)}, u32[]{:S(2)}, u32[]{:S(2)}) %all-to-all-start.3) | async-done | bytes 5079072 | tf_op jit(solution)/shard_map/all_to_all | solution.py:35
  350.7 4.3 fusion.9
  354.9 4.0 fusion.18
  359.2 41.1 %all_to_all.30 = bf16[8,1152,176]{1,2,0:T(8,128)(2,1)S(1)} all-to-all(bf16[8,1152,176]{1,2,0:T(8,128)(2,1)S(1)} %broadcast_in_dim.54), channel_id=1, replica_groups=mesh['yh'=4,'z'=8,'c'=2,'x'=4,'yl'=2] {'x','yl'}, dimensions={0} | all-to-all | bytes 6488064 | tf_op jit(solution)/shard_map/all_to_all | solution.py:35
  400.3 2.0 fusion.8
  402.3 2.1 reshape.586
  404.4 11.4 %all-to-all-start.5 = ((bf16[64,18,256]{2,1,0:T(8,128)(2,1)}), bf16[64,18,256]{2,1,0:T(8,128)(2,1)}, u32[]{:S(2)}, u32[]{:S(2)}) async-start(bf16[64,18,256]{2,1,0:T(8,128)(2,1)} %reshape.586), calls=%async_computation.5 | async-start | bytes 1572864 | tf_op jit(solution)/shard_map/all_to_all | solution.py:181
  417.8 3.5 reshape.585
  421.8 1.0 slice.72
  422.9 1.9 reshape.584
  424.7 15.8 %all-to-all-done.5 = bf16[64,18,256]{2,1,0:T(8,128)(2,1)} async-done(((bf16[64,18,256]{2,1,0:T(8,128)(2,1)}), bf16[64,18,256]{2,1,0:T(8,128)(2,1)}, u32[]{:S(2)}, u32[]{:S(2)}) %all-to-all-start.5) | async-done | bytes 589856 | tf_op jit(solution)/shard_map/all_to_all | solution.py:181
  440.5 1.3 reshape.587
  441.9 2.7 gather_fusion.2
  445.0 2.5 fusion.26
  (85 shorter events, 11.1 us)
Async XLA Ops:
  6.5 393.8 %copy-start = (bf16[1,1408,256]{2,1,0:T(8,128)(2,1)S(1)}, bf16[1,1408,256]{2,1,0:T(8,128)(2,1)}, u32[]{:S(2)}) copy-start(bf16[1,1408,256]{2,1,0:T(8,128)(2,1)} %param.30) | copy-start | bytes 2162692
  6.5 94.5 %all-gather.6.cloned.1.call-start = ((), (), s32[]{:S(2)}) async-start(), calls=%async_computation.7 | async-start | bytes 2433024 | tf_op jit(solution)/shard_map/all_gather | solution.py:68
  11.6 6.1 %copy-start.8 = (bf16[176,32]{0,1:T(8,128)(2,1)S(1)}, bf16[176,32]{0,1:T(8,128)(2,1)}, u32[]{:S(2)}) copy-start(bf16[176,32]{0,1:T(8,128)(2,1)} %param.33) | copy-start | bytes 33796
  11.6 6.1 %copy-start.9 = (bf16[32,176]{1,0:T(8,128)(2,1)S(1)}, bf16[32,176]{1,0:T(8,128)(2,1)}, u32[]{:S(2)}) copy-start(bf16[32,176]{1,0:T(8,128)(2,1)} %param.32) | copy-start | bytes 33796
  11.6 6.1 %copy-start.10 = (bf16[32,176]{1,0:T(8,128)(2,1)S(1)}, bf16[32,176]{1,0:T(8,128)(2,1)}, u32[]{:S(2)}) copy-start(bf16[32,176]{1,0:T(8,128)(2,1)} %param.31) | copy-start | bytes 33796
  11.6 97.0 %copy-start.1 = (s32[64]{0:T(128)S(1)}, s32[64]{0:T(128)}, u32[]{:S(2)}) copy-start(s32[64]{0:T(128)} %param.23) | copy-start | bytes 772
  11.6 206.3 %all-to-all-start.1 = ((bf16[8,128,2048]{2,1,0:T(8,128)(2,1)}), bf16[8,128,2048]{2,1,0:T(8,128)(2,1)}, u32[]{:S(2)}, u32[]{:S(2)}) async-start(bf16[8,128,2048]{2,1,0:T(8,128)(2,1)} %broadcast_in_dim.52), calls=%async_computation.1 | async-start | bytes 8388608 | tf_op jit(solution)/shard_map/all_to_all | solution.py:35
  17.6 166.4 %all-gather.4.cloned.1.call-start = ((), (), s32[]{:S(2)}) async-start(), calls=%async_computation.6 | async-start | bytes 1148928 | tf_op jit(solution)/shard_map/all_gather | solution.py:88
  101.0 92.6 %copy-start.3 = (bf16[9216,128]{1,0:T(8,128)(2,1)S(1)}, bf16[9216,128]{1,0:T(8,128)(2,1)}, u32[]{:S(2)}) copy-start(bf16[9216,128]{1,0:T(8,128)(2,1)} %all-gather.6.cloned.1.call-done) | copy-start | bytes 7077892
  101.0 92.6 %collective-permute-start = (bf16[32,288,128]{2,1,0:T(8,128)(2,1)}, bf16[32,288,128]{2,1,0:T(8,128)(2,1)}, u32[]{:S(2)}, u32[]{:S(2)}) collective-permute-start(bf16[32,288,128]{2,1,0:T(8,128)(2,1)} %bitcast.119), channel_id=1, source_target_pairs={{0,8},{8,0},{1,9},{9,1},{2,10},{10,2},{3,11},{11,3},{4,12},{12,4},... | collective-permute-start | bytes 7077896 | tf_op jit(solution)/shard_map/ppermute | solution.py:69
  185.5 15.1 %collective-permute-start.1 = (bf16[32,132,128]{2,0,1:T(8,128)(2,1)S(1)}, bf16[32,132,128]{2,0,1:T(8,128)(2,1)S(1)}, u32[]{:S(2)}, u32[]{:S(2)}) collective-permute-start(bf16[32,132,128]{2,0,1:T(8,128)(2,1)S(1)} %copy.48), channel_id=1, source_target_pairs={{0,8},{8,0},{1,9},{9,1},{2,10},{10,2},{3,11},{11,3},{4,12},{12,4},... | collective-permute-start | bytes 3244040 | tf_op jit(solution)/shard_map/ppermute | solution.py:89
  193.6 2.2 copy-start.6
  200.2 1.2 copy-start.2
  215.3 6.6 %copy-start.7 = (s32[128,6]{0,1:T(8,128)S(1)}, s32[128,6]{0,1:T(8,128)}, u32[]{:S(2)}) copy-start(s32[128,6]{0,1:T(8,128)} %param.27) | copy-start | bytes 9220
  215.3 7.0 %copy-start.11 = (bf16[2048]{0:T(1024)(128)(2,1)S(1)}, bf16[2048]{0:T(1024)(128)(2,1)}, u32[]{:S(2)}) copy-start(bf16[2048]{0:T(1024)(128)(2,1)} %param.25) | copy-start | bytes 12292
  217.9 18.9 %all-to-all-start = ((bf16[8,480,128]{2,1,0:T(8,128)(2,1)}), bf16[8,480,128]{2,1,0:T(8,128)(2,1)S(1)}, u32[]{:S(2)}, u32[]{:S(2)}) async-start(bf16[8,480,128]{2,1,0:T(8,128)(2,1)} %pad_maximum_fusion.2), calls=%async_computation | async-start | bytes 1966080 | tf_op jit(solution)/shard_map/all_to_all | solution.py:125
  243.4 33.4 %all-to-all-start.2 = ((bf16[64,18,256]{2,1,0:T(8,128)(2,1)}), bf16[64,18,256]{2,1,0:T(8,128)(2,1)}, u32[]{:S(2)}, u32[]{:S(2)}) async-start(bf16[64,18,256]{2,1,0:T(8,128)(2,1)} %reshape.581), calls=%async_computation.2 | async-start | bytes 1572864 | tf_op jit(solution)/shard_map/all_to_all | solution.py:162
  282.5 68.2 %all-to-all-start.3 = ((bf16[8,1240,256]{2,1,0:T(8,128)(2,1)}), bf16[8,1240,256]{2,1,0:T(8,128)(2,1)}, u32[]{:S(2)}, u32[]{:S(2)}) async-start(bf16[8,1240,256]{2,1,0:T(8,128)(2,1)} %broadcast_in_dim.53), calls=%async_computation.3 | async-start | bytes 10158080 | tf_op jit(solution)/shard_map/all_to_all | solution.py:35
  350.7 4.3 copy-start.4
  402.3 19.0 %copy-start.5 = (bf16[2048,64]{0,1:T(8,128)(2,1)S(1)}, bf16[2048,64]{0,1:T(8,128)(2,1)}, u32[]{:S(2)}) copy-start(bf16[2048,64]{0,1:T(8,128)(2,1)} %param.26) | copy-start | bytes 786436
  404.4 36.1 %all-to-all-start.5 = ((bf16[64,18,256]{2,1,0:T(8,128)(2,1)}), bf16[64,18,256]{2,1,0:T(8,128)(2,1)}, u32[]{:S(2)}, u32[]{:S(2)}) async-start(bf16[64,18,256]{2,1,0:T(8,128)(2,1)} %reshape.586), calls=%async_computation.5 | async-start | bytes 1572864 | tf_op jit(solution)/shard_map/all_to_all | solution.py:181
Sparse Core Ops, SparseCore 0:
  10.5 90.4 all-gather.5
  108.6 75.3 all-gather.3

commit v2 on v0

--- a/solution.py
+++ b/solution.py
@@ -1,3 +1,4 @@
+import functools
 import math
 
 import jax
@@ -70,46 +71,48 @@
         [key_cache, key_new, value_cache, value_new, wpack.reshape(w_rows, HD)], 0
     )
     g = lax.all_gather(kv, "yh", axis=0)
-    g = lax.all_gather(g, "z", axis=0)
+    g = lax.all_gather(g, "z", axis=0).reshape(n_z * n_yh, kv.shape[0], HD)
     other = lax.ppermute(g, "c", [(0, 1), (1, 0)])
-    kvg = jnp.stack([g, other], 0).reshape(n_seq, kv.shape[0], HD)
     my_c = lax.axis_index("c")
-    pos = jnp.arange(n_seq, dtype=jnp.int32)
-    src = (pos % n_yh) * (n_z * n_c) + ((pos // n_yh) % n_z) * n_c + (pos // (n_yh * n_z) + my_c) % n_c
-    s_ids = jnp.arange(n_seq, dtype=jnp.int32)
-    pos_of_s = ((s_ids % n_c - my_c) % n_c) * (n_yh * n_z) + ((s_ids // n_c) % n_z) * n_yh + s_ids // (n_c * n_z)
     kv_rows = 2 * (block_rows + tok_rows)
-    wg = jnp.take(kvg[:, kv_rows:], pos_of_s, axis=0).reshape(n_seq, 3, wpack.shape[1], wpack.shape[2])
+    first = my_c == 0
+    w_c0 = jnp.where(first, g[:, kv_rows:], other[:, kv_rows:])
+    w_c1 = jnp.where(first, other[:, kv_rows:], g[:, kv_rows:])
+    wk = jnp.stack([w_c0, w_c1], 0).reshape(n_c, n_z, n_yh, w_rows, HD)
+    wg = jnp.transpose(wk, (2, 1, 0, 3, 4)).reshape(n_seq, 3, wpack.shape[1], wpack.shape[2])
     sg_w = wg[:, 0].reshape(n_seq * wpack.shape[1], wpack.shape[2])
     su_w = wg[:, 1].reshape(n_seq * wpack.shape[1], wpack.shape[2])
     sd_t = wg[:, 2].reshape(n_tp, n_seq // n_tp, wpack.shape[1], wpack.shape[2])
     ow_all = tp_gather(out_weight, n_tp)
-    ck = kvg[:, :block_rows].reshape(n_seq * block_rows, HD)
-    nk = kvg[:, block_rows:block_rows + tok_rows].reshape(n_seq * tok_rows, HD)
-    cv = kvg[:, block_rows + tok_rows:2 * block_rows + tok_rows].reshape(n_seq * block_rows, HD)
-    nv = kvg[:, 2 * block_rows + tok_rows:kv_rows].reshape(n_seq * tok_rows, HD)
 
     scale = 1.0 / math.sqrt(HD)
-    s_c = jnp.dot(query, ck.T, preferred_element_type=jnp.float32) * scale
-    s_n = jnp.dot(query, nk.T, preferred_element_type=jnp.float32) * scale
-    c_open = (
-        jnp.arange(block_rows, dtype=jnp.int32)[None, :] < cache_len[src][:, None]
-    ).reshape(n_seq * block_rows)
-    key_place = (src[:, None] * tok_rows + jnp.arange(tok_rows, dtype=jnp.int32)[None, :]).reshape(
-        n_seq * tok_rows
-    )
+    pos = jnp.arange(n_z * n_yh, dtype=jnp.int32)
     query_place = seq_index * tok_rows + jnp.arange(tok_rows, dtype=jnp.int32)
-    n_open = key_place[None, :] <= query_place[:, None]
-    s_c = jnp.where(c_open[None, :], s_c, -jnp.inf)
-    s_n = jnp.where(n_open, s_n, -jnp.inf)
-    top = jnp.maximum(jnp.max(s_c, axis=-1, keepdims=True), jnp.max(s_n, axis=-1, keepdims=True))
-    e_c = jnp.exp(s_c - top)
-    e_n = jnp.exp(s_n - top)
-    total = jnp.sum(e_c, axis=-1, keepdims=True) + jnp.sum(e_n, axis=-1, keepdims=True)
-    p_c = (e_c / total).astype(jnp.bfloat16)
-    p_n = (e_n / total).astype(jnp.bfloat16)
-    attn = jnp.dot(p_c, cv, preferred_element_type=jnp.float32) + jnp.dot(
-        p_n, nv, preferred_element_type=jnp.float32
+    halves = []
+    for part, c_of in ((g, my_c), (other, 1 - my_c)):
+        src = (pos % n_yh) * (n_z * n_c) + (pos // n_yh) * n_c + c_of
+        ck = part[:, :block_rows].reshape(-1, HD)
+        nk = part[:, block_rows:block_rows + tok_rows].reshape(-1, HD)
+        cv = part[:, block_rows + tok_rows:2 * block_rows + tok_rows].reshape(-1, HD)
+        nv = part[:, 2 * block_rows + tok_rows:kv_rows].reshape(-1, HD)
+        s_c = jnp.dot(query, ck.T, preferred_element_type=jnp.float32) * scale
+        s_n = jnp.dot(query, nk.T, preferred_element_type=jnp.float32) * scale
+        c_open = (
+            jnp.arange(block_rows, dtype=jnp.int32)[None, :] < cache_len[src][:, None]
+        ).reshape(-1)
+        key_place = (src[:, None] * tok_rows + jnp.arange(tok_rows, dtype=jnp.int32)[None, :]).reshape(-1)
+        s_c = jnp.where(c_open[None, :], s_c, -jnp.inf)
+        s_n = jnp.where(key_place[None, :] <= query_place[:, None], s_n, -jnp.inf)
+        halves.append((s_c, s_n, cv, nv))
+    top = functools.reduce(
+        jnp.maximum, [jnp.max(x, axis=-1, keepdims=True) for h in halves for x in h[:2]]
+    )
+    exps = [(jnp.exp(h[0] - top), jnp.exp(h[1] - top)) for h in halves]
+    total = sum(jnp.sum(x, axis=-1, keepdims=True) for e in exps for x in e)
+    attn = sum(
+        jnp.dot((e_c / total).astype(jnp.bfloat16), h[2], preferred_element_type=jnp.float32)
+        + jnp.dot((e_n / total).astype(jnp.bfloat16), h[3], preferred_element_type=jnp.float32)
+        for (e_c, e_n), h in zip(exps, halves)
     )
     attn = attn.astype(jnp.bfloat16)
 

time: 388 us -> 389 us (level)
  waiting for transfers between devices: 171 us -> 165 us
  matrix products: 23.7 us -> 28.1 us
    gather x2 -> x0, local copies, waits for them, and re-layouts: 8.5 us -> none  [local(): jnp.take(kvg[:, kv_rows:], pos_of_s, axis=0)]
    reshape x0 -> x1, local copies, waits for them, and re-layouts: none -> 5.86 us  [local(): jnp.transpose(wk, (2, 1, 0, 3, 4))]
    all_to_all x2, waiting for transfers between devices: 68.5 us -> 63.2 us  [tp_gather(): return lax.all_to_all(b, TP, split_axis=0, concat_axis=0, tiled=True)]
    another operation x2 -> x0, local copies, waits for them, and re-layouts: 4.22 us -> none  [local(): kvg = jnp.stack([g, other], 0).reshape(n_seq, kv.shape[0], HD)]
    slice x4 -> x5, local copies, waits for them, and re-layouts: 5.6 us -> 8.5 us  [the longest x2 5.59 us: local(): nv = part[:, 2 * block_rows + tok_rows:kv_rows].reshape(-1, HD)]
    unnamed x25 -> x57, local copies, waits for them, and re-layouts: 10.3 us -> 12.9 us
  transfers between devices with their start and end apart: 7 -> 7, of which waited for: 6 -> 6; matrix products, arithmetic and copies ran while one was open for 14% -> 16% of each run, Pallas kernels for 0% -> 0%
where the time goes in v2:
time: 389 us; the launch traced here: 387 us
  waiting for transfers between devices  165 us (42%)
  local copies, waits for them, and re-layouts  65.4 us (17%)
  blocking collectives  58.3 us (15%)
  starting transfers between devices  43.8 us (11%)
  matrix products  28.1 us (7%)
  between operations  13.9 us (4%)
  other arithmetic  12.4 us (3%)
    all_to_all x2, waiting for transfers between devices, tp_gather(): return lax.all_to_all(b, TP, split_axis=0, concat_axis=0, tiled=True)  63.2 us
    all_gather x1, waiting for transfers between devices, local(): g = lax.all_gather(g, 'z', axis=0).reshape(n_z * n_yh, kv.shape[0], HD)  56.6 us
    all_to_all x1, blocking collectives, tp_gather(): return lax.all_to_all(b, TP, split_axis=0, concat_axis=0, tiled=True)  41.1 us
    all_to_all x1, waiting for transfers between devices, local(): recv = lax.all_to_all(buffer, SEQ, split_axis=0, concat_axis=0, tiled=True)  20.4 us
    all_gather x1, blocking collectives, local(): g = lax.all_gather(kv, 'yh', axis=0)  17.2 us
    all_to_all x1, waiting for transfers between devices, local(): returned = lax.all_to_all(out, SEQ, split_axis=0, concat_axis=0, tiled=True)  15.8 us
    all_to_all x2, starting transfers between devices, tp_gather(): return lax.all_to_all(b, TP, split_axis=0, concat_axis=0, tiled=True)  14.2 us
    unnamed x57, local copies, waits for them, and re-layouts  12.9 us
  transfers between devices with their start and end apart: 7, of which 6 were waited for; matrix products, arithmetic and copies ran while one was open for 16% of the time, Pallas kernels for 0%

profile of v2, /device:TPU:1, one launch (start us, length us, event | category | flops | bytes accessed | tf_op | source)
XLA Modules:
  0.0 387.2 jit_solution(10407411667001875815)
XLA Ops:
  10.4 17.2 %all-gather.2 = bf16[4,420,128]{2,1,0:T(8,128)(2,1)} all-gather(bf16[1,420,128]{2,1,0:T(8,128)(2,1)S(1)} %bitcast.138), channel_id=2, replica_groups=mesh['yh'=4,'z'=8,'c'=2,'x'=4,'yl'=2] {'yh'}, dimensions={0}, use_global_device_ids=true | all-gather | bytes 537600 | tf_op jit(solution)/shard_map/all_gather | solution.py:73
  27.6 56.6 %all-gather.5.cloned.1.call-done = bf16[32,420,128]{2,1,0:T(8,128)(2,1)} async-done(((bf16[4,420,128]{2,1,0:T(8,128)(2,1)}), bf16[32,420,128]{2,1,0:T(8,128)(2,1)}) %all-gather.5.cloned.1.call-update) | async-done | bytes 3440656 | tf_op jit(solution)/shard_map/all_gather | solution.py:74
  84.3 4.3 %copy.81 = bf16[32,420,128]{2,0,1:T(8,128)(2,1)} copy(bf16[32,420,128]{2,1,0:T(8,128)(2,1)} %all-gather.5.cloned.1.call-done) | data formatting | bytes 6881280 | tf_op jit(solution)/shard_map/all_gather | solution.py:74
  88.5 2.7 collective-permute-start
  91.3 2.5 broadcast_in_dim.44
  93.8 5.0 %all-to-all-start.1 = ((bf16[8,128,2048]{2,1,0:T(8,128)(2,1)}), bf16[8,128,2048]{2,1,0:T(8,128)(2,1)}, u32[]{:S(2)}, u32[]{:S(2)}) async-start(bf16[8,128,2048]{2,1,0:T(8,128)(2,1)} %broadcast_in_dim.44), calls=%async_computation.1 | async-start | bytes 8388608 | tf_op jit(solution)/shard_map/all_to_all | solution.py:36
  101.3 1.6 fusion.61
  103.0 1.4 fusion.67
  104.4 2.7 fusion.60
  107.1 3.5 fusion.68
  110.6 1.7 broadcast_select_fusion.1
  112.3 1.5 maximum_bitcast_fusion
  114.7 2.9 fusion.63
  117.6 1.4 copy.105
  121.3 5.9 %reshape.357 = bf16[64,3,32,176]{3,2,1,0:T(8,128)(2,1)} reshape(bf16[4,8,2,132,128]{4,3,2,1,0:T(8,128)(2,1)S(1)} %copy.87) | data formatting | bytes 4325376 | tf_op jit(solution)/shard_map/reshape | solution.py:82
  127.2 3.6 fusion.64
  130.8 1.5 reshape_reshape_squeeze.3
  139.6 8.6 %all-to-all-done.1 = bf16[8,128,2048]{2,1,0:T(8,128)(2,1)} async-done(((bf16[8,128,2048]{2,1,0:T(8,128)(2,1)}), bf16[8,128,2048]{2,1,0:T(8,128)(2,1)}, u32[]{:S(2)}, u32[]{:S(2)}) %all-to-all-start.1) | async-done | bytes 4194336 | tf_op jit(solution)/shard_map/all_to_all | solution.py:36
  148.2 3.7 all-to-all-start
  152.4 1.8 reduce-window.6
  156.1 9.3 %all-to-all-done = bf16[8,480,128]{2,1,0:T(8,128)(2,1)S(1)} async-done(((bf16[8,480,128]{2,1,0:T(8,128)(2,1)}), bf16[8,480,128]{2,1,0:T(8,128)(2,1)S(1)}, u32[]{:S(2)}, u32[]{:S(2)}) %all-to-all-start) | async-done | bytes 983072 | tf_op jit(solution)/shard_map/all_to_all | solution.py:123
  165.4 3.1 multiply_reduce_fusion.1
  168.7 1.1 convolution_convert_fusion
  169.8 2.1 reshape.359
  171.9 11.9 %all-to-all-start.2 = ((bf16[64,18,256]{2,1,0:T(8,128)(2,1)}), bf16[64,18,256]{2,1,0:T(8,128)(2,1)}, u32[]{:S(2)}, u32[]{:S(2)}) async-start(bf16[64,18,256]{2,1,0:T(8,128)(2,1)} %reshape.359), calls=%async_computation.2 | async-start | bytes 1572864 | tf_op jit(solution)/shard_map/all_to_all | solution.py:160
  183.8 1.7 fusion.69
  185.5 1.7 fusion.30
  187.6 20.4 %all-to-all-done.2 = bf16[64,18,256]{2,1,0:T(8,128)(2,1)} async-done(((bf16[64,18,256]{2,1,0:T(8,128)(2,1)}), bf16[64,18,256]{2,1,0:T(8,128)(2,1)}, u32[]{:S(2)}, u32[]{:S(2)}) %all-to-all-start.2) | async-done | bytes 589856 | tf_op jit(solution)/shard_map/all_to_all | solution.py:160
  208.0 2.1 reshape.360
  210.1 1.1 pad_maximum_fusion.1
  211.2 2.6 broadcast_in_dim.45
  213.8 9.2 %all-to-all-start.3 = ((bf16[8,1240,256]{2,1,0:T(8,128)(2,1)}), bf16[8,1240,256]{2,1,0:T(8,128)(2,1)}, u32[]{:S(2)}, u32[]{:S(2)}) async-start(bf16[8,1240,256]{2,1,0:T(8,128)(2,1)} %broadcast_in_dim.45), calls=%async_computation.3 | async-start | bytes 10158080 | tf_op jit(solution)/shard_map/all_to_all | solution.py:36
  223.0 2.2 copy.107
  225.1 2.2 copy.108
  227.3 54.7 %all-to-all-done.3 = bf16[8,1240,256]{2,1,0:T(8,128)(2,1)} async-done(((bf16[8,1240,256]{2,1,0:T(8,128)(2,1)}), bf16[8,1240,256]{2,1,0:T(8,128)(2,1)}, u32[]{:S(2)}, u32[]{:S(2)}) %all-to-all-start.3) | async-done | bytes 5079072 | tf_op jit(solution)/shard_map/all_to_all | solution.py:36
  281.9 4.3 %fusion.10 = f32[1152,176]{0,1:T(8,128)S(1)} fusion(bf16[8,1240,256]{2,1,0:T(8,128)(2,1)} %all-to-all-done.3, bf16[8,256,176]{1,0,2:T(8,128)(2,1)} %bitcast.133), kind=kOutput, calls=%fused_computation.18 | convolution fusion | flops 830472192 | bytes 6250496 | tf_op jit(solution)/shard_map/tsc,tcf->sf/dot_general | solution.py:172
  286.2 4.0 %fusion.19 = bf16[1152,176]{0,1:T(8,128)(2,1)S(1)} fusion(bf16[8,1240,256]{2,1,0:T(8,128)(2,1)} %all-to-all-done.3, f32[1152,176]{0,1:T(8,128)S(1)} %fusion.10, bf16[8,256,176]{1,0,2:T(8,128)(2,1)S(1)} %bitcast.132), kind=kOutput, calls=%fused_computation.21 | convolution fusion | flops 831688704 | bytes 6656000 | tf_op jit(solution)/shard_map/tsc,tcf->sf/dot_general | solution.py:173
  290.5 41.1 %all_to_all.30 = bf16[8,1152,176]{1,2,0:T(8,128)(2,1)S(1)} all-to-all(bf16[8,1152,176]{1,2,0:T(8,128)(2,1)S(1)} %broadcast_in_dim.46), channel_id=1, replica_groups=mesh['yh'=4,'z'=8,'c'=2,'x'=4,'yl'=2] {'x','yl'}, dimensions={0} | all-to-all | bytes 6488064 | tf_op jit(solution)/shard_map/all_to_all | solution.py:36
  331.6 2.0 fusion.9
  333.6 2.1 reshape.364
  335.6 11.2 %all-to-all-start.5 = ((bf16[64,18,256]{2,1,0:T(8,128)(2,1)}), bf16[64,18,256]{2,1,0:T(8,128)(2,1)}, u32[]{:S(2)}, u32[]{:S(2)}) async-start(bf16[64,18,256]{2,1,0:T(8,128)(2,1)} %reshape.364), calls=%async_computation.5 | async-start | bytes 1572864 | tf_op jit(solution)/shard_map/all_to_all | solution.py:179
  348.8 3.5 reshape.363
  353.8 1.9 reshape.362
  355.7 15.8 %all-to-all-done.5 = bf16[64,18,256]{2,1,0:T(8,128)(2,1)} async-done(((bf16[64,18,256]{2,1,0:T(8,128)(2,1)}), bf16[64,18,256]{2,1,0:T(8,128)(2,1)}, u32[]{:S(2)}, u32[]{:S(2)}) %all-to-all-start.5) | async-done | bytes 589856 | tf_op jit(solution)/shard_map/all_to_all | solution.py:179
  371.5 1.3 reshape.365
  372.8 2.7 gather_fusion.2
  376.6 1.6 multiply_reduce_fusion
  378.2 2.2 fusion.29
  (116 shorter events, 24.2 us)
Async XLA Ops:
  6.5 325.1 %copy-start = (bf16[1,1408,256]{2,1,0:T(8,128)(2,1)S(1)}, bf16[1,1408,256]{2,1,0:T(8,128)(2,1)}, u32[]{:S(2)}) copy-start(bf16[1,1408,256]{2,1,0:T(8,128)(2,1)} %param.30) | copy-start | bytes 2162692
  6.5 77.7 %all-gather.5.cloned.1.call-start = ((), (), s32[]{:S(2)}) async-start(), calls=%async_computation.6 | async-start | bytes 3907584 | tf_op jit(solution)/shard_map/all_gather | solution.py:74
  27.6 63.7 %copy-start.9 = (bf16[128,2048]{1,0:T(8,128)(2,1)S(1)}, bf16[128,2048]{1,0:T(8,128)(2,1)}, u32[]{:S(2)}) copy-start(bf16[128,2048]{1,0:T(8,128)(2,1)} %param.24) | copy-start | bytes 1572868
  88.5 22.1 %collective-permute-start = (bf16[32,420,128]{2,0,1:T(8,128)(2,1)}, bf16[32,420,128]{2,0,1:T(8,128)(2,1)}, u32[]{:S(2)}, u32[]{:S(2)}) collective-permute-start(bf16[32,420,128]{2,0,1:T(8,128)(2,1)} %copy.81), channel_id=1, source_target_pairs={{0,8},{8,0},{1,9},{9,1},{2,10},{10,2},{3,11},{11,3},{4,12},{12,4},... | collective-permute-start | bytes 10321928 | tf_op jit(solution)/shard_map/ppermute | solution.py:75
  93.8 5.1 %copy-start.1 = (s32[64]{0:T(128)S(1)}, s32[64]{0:T(128)}, u32[]{:S(2)}) copy-start(s32[64]{0:T(128)} %param.23) | copy-start | bytes 772
  93.8 9.1 %copy-start.14 = (bf16[128,128]{1,0:T(8,128)(2,1)S(1)}, bf16[128,128]{1,0:T(8,128)(2,1)}, u32[]{:S(2)}) copy-start(bf16[128,128]{1,0:T(8,128)(2,1)} %param.18) | copy-start | bytes 98308
  93.8 54.4 %all-to-all-start.1 = ((bf16[8,128,2048]{2,1,0:T(8,128)(2,1)}), bf16[8,128,2048]{2,1,0:T(8,128)(2,1)}, u32[]{:S(2)}, u32[]{:S(2)}) async-start(bf16[8,128,2048]{2,1,0:T(8,128)(2,1)} %broadcast_in_dim.44), calls=%async_computation.1 | async-start | bytes 8388608 | tf_op jit(solution)/shard_map/all_to_all | solution.py:36
  101.2 5.9 %copy-start.21 = (s32[128]{0:T(128)}, s32[128]{0:T(128)S(1)}, u32[]{:S(2)}) copy-start(s32[128]{0:T(128)S(1)} %iota_add_fusion) | copy-start | bytes 1540
  130.8 1.5 copy-start.3
  132.3 0.9 copy-start.10
  132.3 0.9 copy-start.15
  132.3 0.9 copy-start.18
  132.3 1.1 copy-start.22
  132.7 1.6 copy-start.19
  132.7 1.6 copy-start.20
  132.8 1.6 copy-start.6
  133.2 1.6 copy-start.4
  134.8 0.9 copy-start.13
  134.8 1.3 copy-start.5
  136.1 1.2 copy-start.7
  137.3 0.9 copy-start.12
  138.5 13.5 %copy-start.16 = (s32[128,6]{0,1:T(8,128)S(1)}, s32[128,6]{0,1:T(8,128)}, u32[]{:S(2)}) copy-start(s32[128,6]{0,1:T(8,128)} %param.27) | copy-start | bytes 9220
  138.5 13.8 %copy-start.17 = (bf16[2048]{0:T(1024)(128)(2,1)S(1)}, bf16[2048]{0:T(1024)(128)(2,1)}, u32[]{:S(2)}) copy-start(bf16[2048]{0:T(1024)(128)(2,1)} %param.25) | copy-start | bytes 12292
  148.2 17.1 %all-to-all-start = ((bf16[8,480,128]{2,1,0:T(8,128)(2,1)}), bf16[8,480,128]{2,1,0:T(8,128)(2,1)S(1)}, u32[]{:S(2)}, u32[]{:S(2)}) async-start(bf16[8,480,128]{2,1,0:T(8,128)(2,1)} %pad_maximum_fusion), calls=%async_computation | async-start | bytes 1966080 | tf_op jit(solution)/shard_map/all_to_all | solution.py:123
  171.9 36.1 %all-to-all-start.2 = ((bf16[64,18,256]{2,1,0:T(8,128)(2,1)}), bf16[64,18,256]{2,1,0:T(8,128)(2,1)}, u32[]{:S(2)}, u32[]{:S(2)}) async-start(bf16[64,18,256]{2,1,0:T(8,128)(2,1)} %reshape.359), calls=%async_computation.2 | async-start | bytes 1572864 | tf_op jit(solution)/shard_map/all_to_all | solution.py:160
  213.8 68.2 %all-to-all-start.3 = ((bf16[8,1240,256]{2,1,0:T(8,128)(2,1)}), bf16[8,1240,256]{2,1,0:T(8,128)(2,1)}, u32[]{:S(2)}, u32[]{:S(2)}) async-start(bf16[8,1240,256]{2,1,0:T(8,128)(2,1)} %broadcast_in_dim.45), calls=%async_computation.3 | async-start | bytes 10158080 | tf_op jit(solution)/shard_map/all_to_all | solution.py:36
  281.9 4.3 %copy-start.8 = (bf16[22,8,8,256]{3,2,1,0:T(8,128)(2,1)S(1)}, bf16[22,8,8,256]{3,2,1,0:T(8,128)(2,1)}, u32[]{:S(2)}) copy-start(bf16[22,8,8,256]{3,2,1,0:T(8,128)(2,1)} %copy.108) | copy-start | bytes 2162692
  335.6 16.6 %copy-start.11 = (bf16[2048,64]{0,1:T(8,128)(2,1)S(1)}, bf16[2048,64]{0,1:T(8,128)(2,1)}, u32[]{:S(2)}) copy-start(bf16[2048,64]{0,1:T(8,128)(2,1)} %param.26) | copy-start | bytes 786436
  335.6 35.8 %all-to-all-start.5 = ((bf16[64,18,256]{2,1,0:T(8,128)(2,1)}), bf16[64,18,256]{2,1,0:T(8,128)(2,1)}, u32[]{:S(2)}, u32[]{:S(2)}) async-start(bf16[64,18,256]{2,1,0:T(8,128)(2,1)} %reshape.364), calls=%async_computation.5 | async-start | bytes 1572864 | tf_op jit(solution)/shard_map/all_to_all | solution.py:179
  375.5 2.7 copy-start.2
Sparse Core Ops, SparseCore 0:
  27.7 56.4 all-gather.4

commit v3 on v0

--- a/solution.py
+++ b/solution.py
@@ -2,10 +2,10 @@
 
 import jax
 import jax.numpy as jnp
-import numpy as np
 from jax import lax
 from jax.sharding import Mesh
 from jax.sharding import PartitionSpec as P
+
 
 D = 2048
 HD = 128
@@ -14,20 +14,6 @@
 
 SEQ = ("yh", "z", "c")
 TP = ("x", "yl")
-
-
-def gather_seq(x):
-    g = lax.all_gather(x, "yh", axis=0)
-    g = lax.all_gather(g, "z", axis=0)
-    g = lax.all_gather(g, "c", axis=0)
-    return g
-
-
-def tp_blocks(x, n_tp):
-    out = [x]
-    for k in range(1, n_tp):
-        out.append(lax.ppermute(x, TP, [(j, (j + k) % n_tp) for j in range(n_tp)]))
-    return out
 
 
 def tp_gather(x, n_tp):

time: 388 us -> 388 us (level)
  no operation moved by 1% of the time
where the time goes in v3:
time: 388 us; the launch traced here: 387 us
  waiting for transfers between devices  171 us (44%)
  local copies, waits for them, and re-layouts  62.7 us (16%)
  blocking collectives  58.3 us (15%)
  starting transfers between devices  44.3 us (11%)
  matrix products  23.7 us (6%)
  between operations  13.8 us (4%)
  other arithmetic  13.1 us (3%)
    all_to_all x2, waiting for transfers between devices, tp_gather(): return lax.all_to_all(b, TP, split_axis=0, concat_axis=0, tiled=True)  68.5 us
    all_gather x1, waiting for transfers between devices, local(): g = lax.all_gather(g, 'z', axis=0)  56.6 us
    all_to_all x1, blocking collectives, tp_gather(): return lax.all_to_all(b, TP, split_axis=0, concat_axis=0, tiled=True)  41.1 us
    all_to_all x1, waiting for transfers between devices, local(): recv = lax.all_to_all(buffer, SEQ, split_axis=0, concat_axis=0, tiled=True)  20.5 us
    all_gather x1, blocking collectives, local(): g = lax.all_gather(kv, 'yh', axis=0)  17.2 us
    all_to_all x1, waiting for transfers between devices, local(): returned = lax.all_to_all(out, SEQ, split_axis=0, concat_axis=0, tiled=True)  15.8 us
    all_to_all x2, starting transfers between devices, tp_gather(): return lax.all_to_all(b, TP, split_axis=0, concat_axis=0, tiled=True)  14.5 us
    all_to_all x1, starting transfers between devices, local(): recv = lax.all_to_all(buffer, SEQ, split_axis=0, concat_axis=0, tiled=True)  11.9 us
  transfers between devices with their start and end apart: 7, of which 6 were waited for; matrix products, arithmetic and copies ran while one was open for 14% of the time, Pallas kernels for 0%

profile of v3, /device:TPU:1, one launch (start us, length us, event | category | flops | bytes accessed | tf_op | source)
XLA Modules:
  0.0 386.5 jit_solution(3856518325411960046)
XLA Ops:
  10.4 17.2 %all-gather.2 = bf16[4,420,128]{2,1,0:T(8,128)(2,1)} all-gather(bf16[1,420,128]{2,1,0:T(8,128)(2,1)S(1)} %bitcast.121), channel_id=2, replica_groups=mesh['yh'=4,'z'=8,'c'=2,'x'=4,'yl'=2] {'yh'}, dimensions={0}, use_global_device_ids=true | all-gather | bytes 537600 | tf_op jit(solution)/shard_map/all_gather | solution.py:58
  27.6 56.6 %all-gather.5.cloned.1.call-done = bf16[32,420,128]{2,1,0:T(8,128)(2,1)} async-done(((bf16[4,420,128]{2,1,0:T(8,128)(2,1)}), bf16[32,420,128]{2,1,0:T(8,128)(2,1)}) %all-gather.5.cloned.1.call-update) | async-done | bytes 3440656 | tf_op jit(solution)/shard_map/all_gather | solution.py:59
  84.3 5.1 %copy.63 = bf16[8,4,420,128]{3,0,2,1:T(8,128)(2,1)} copy(bf16[8,4,420,128]{3,2,1,0:T(8,128)(2,1)} %bitcast.108) | data formatting | bytes 6881280 | tf_op jit(solution)/shard_map/all_gather | solution.py:59
  89.4 2.7 collective-permute-start
  92.1 2.6 broadcast_in_dim.52
  94.7 5.0 %all-to-all-start.1 = ((bf16[8,128,2048]{2,1,0:T(8,128)(2,1)}), bf16[8,128,2048]{2,1,0:T(8,128)(2,1)}, u32[]{:S(2)}, u32[]{:S(2)}) async-start(bf16[8,128,2048]{2,1,0:T(8,128)(2,1)} %broadcast_in_dim.52), calls=%async_computation.1 | async-start | bytes 8388608 | tf_op jit(solution)/shard_map/all_to_all | solution.py:21
  100.9 3.3 copy.64
  104.2 2.6 pad_maximum_fusion
  107.8 2.8 copy-done.2
  110.6 1.5 slice.66
  112.1 2.6 gather_fusion.1
  114.7 5.9 %gather.14 = bf16[64,3,32,176]{3,2,1,0:T(8,128)(2,1)} reshape(bf16[64,132,128]{2,1,0:T(8,128)(2,1)S(1)} %gather_fusion.1) | data formatting | bytes 4325376 | tf_op jit(solution)/shard_map/jit(_take)/gather | solution.py:68
  120.6 2.2 broadcast_select_fusion
  122.8 1.6 fusion.78
  124.5 1.5 reshape_reshape_squeeze.3
  127.4 2.7 fusion.77
  130.1 1.3 fusion.80
  131.6 1.1 fusion.6
  135.1 14.1 %all-to-all-done.1 = bf16[8,128,2048]{2,1,0:T(8,128)(2,1)} async-done(((bf16[8,128,2048]{2,1,0:T(8,128)(2,1)}), bf16[8,128,2048]{2,1,0:T(8,128)(2,1)}, u32[]{:S(2)}, u32[]{:S(2)}) %all-to-all-start.1) | async-done | bytes 4194336 | tf_op jit(solution)/shard_map/all_to_all | solution.py:21
  149.1 3.8 all-to-all-start
  153.4 1.8 reduce-window.6
  157.1 9.2 %all-to-all-done = bf16[8,480,128]{2,1,0:T(8,128)(2,1)S(1)} async-done(((bf16[8,480,128]{2,1,0:T(8,128)(2,1)}), bf16[8,480,128]{2,1,0:T(8,128)(2,1)S(1)}, u32[]{:S(2)}, u32[]{:S(2)}) %all-to-all-start) | async-done | bytes 983072 | tf_op jit(solution)/shard_map/all_to_all | solution.py:106
  166.3 3.1 multiply_reduce_fusion.1
  169.6 1.1 convolution_convert_fusion
  170.7 2.1 reshape.528
  172.8 11.9 %all-to-all-start.2 = ((bf16[64,18,256]{2,1,0:T(8,128)(2,1)}), bf16[64,18,256]{2,1,0:T(8,128)(2,1)}, u32[]{:S(2)}, u32[]{:S(2)}) async-start(bf16[64,18,256]{2,1,0:T(8,128)(2,1)} %reshape.528), calls=%async_computation.2 | async-start | bytes 1572864 | tf_op jit(solution)/shard_map/all_to_all | solution.py:143
  184.7 1.7 fusion.81
  186.5 1.7 fusion.27
  188.5 20.5 %all-to-all-done.2 = bf16[64,18,256]{2,1,0:T(8,128)(2,1)} async-done(((bf16[64,18,256]{2,1,0:T(8,128)(2,1)}), bf16[64,18,256]{2,1,0:T(8,128)(2,1)}, u32[]{:S(2)}, u32[]{:S(2)}) %all-to-all-start.2) | async-done | bytes 589856 | tf_op jit(solution)/shard_map/all_to_all | solution.py:143
  208.9 2.1 reshape.529
  211.0 1.1 pad_maximum_fusion.2
  212.1 2.6 broadcast_in_dim.53
  214.7 9.4 %all-to-all-start.3 = ((bf16[8,1240,256]{2,1,0:T(8,128)(2,1)}), bf16[8,1240,256]{2,1,0:T(8,128)(2,1)}, u32[]{:S(2)}, u32[]{:S(2)}) async-start(bf16[8,1240,256]{2,1,0:T(8,128)(2,1)} %broadcast_in_dim.53), calls=%async_computation.3 | async-start | bytes 10158080 | tf_op jit(solution)/shard_map/all_to_all | solution.py:21
  224.1 2.2 copy.81
  226.3 2.2 copy.82
  228.5 54.4 %all-to-all-done.3 = bf16[8,1240,256]{2,1,0:T(8,128)(2,1)} async-done(((bf16[8,1240,256]{2,1,0:T(8,128)(2,1)}), bf16[8,1240,256]{2,1,0:T(8,128)(2,1)}, u32[]{:S(2)}, u32[]{:S(2)}) %all-to-all-start.3) | async-done | bytes 5079072 | tf_op jit(solution)/shard_map/all_to_all | solution.py:21
  282.9 4.3 %fusion.9 = f32[1152,176]{0,1:T(8,128)S(1)} fusion(bf16[8,1240,256]{2,1,0:T(8,128)(2,1)} %all-to-all-done.3, bf16[8,256,176]{1,0,2:T(8,128)(2,1)} %bitcast.119), kind=kOutput, calls=%fused_computation.20 | convolution fusion | flops 830472192 | bytes 6250496 | tf_op jit(solution)/shard_map/tsc,tcf->sf/dot_general | solution.py:155
  287.2 4.0 %fusion.18 = bf16[1152,176]{0,1:T(8,128)(2,1)S(1)} fusion(bf16[8,1240,256]{2,1,0:T(8,128)(2,1)} %all-to-all-done.3, f32[1152,176]{0,1:T(8,128)S(1)} %fusion.9, bf16[8,256,176]{1,0,2:T(8,128)(2,1)S(1)} %bitcast.118), kind=kOutput, calls=%fused_computation.23 | convolution fusion | flops 831688704 | bytes 6656000 | tf_op jit(solution)/shard_map/tsc,tcf->sf/dot_general | solution.py:156
  291.4 41.1 %all_to_all.30 = bf16[8,1152,176]{1,2,0:T(8,128)(2,1)S(1)} all-to-all(bf16[8,1152,176]{1,2,0:T(8,128)(2,1)S(1)} %broadcast_in_dim.54), channel_id=1, replica_groups=mesh['yh'=4,'z'=8,'c'=2,'x'=4,'yl'=2] {'x','yl'}, dimensions={0} | all-to-all | bytes 6488064 | tf_op jit(solution)/shard_map/all_to_all | solution.py:21
  332.6 2.0 fusion.8
  334.5 2.1 reshape.533
  336.6 11.4 %all-to-all-start.5 = ((bf16[64,18,256]{2,1,0:T(8,128)(2,1)}), bf16[64,18,256]{2,1,0:T(8,128)(2,1)}, u32[]{:S(2)}, u32[]{:S(2)}) async-start(bf16[64,18,256]{2,1,0:T(8,128)(2,1)} %reshape.533), calls=%async_computation.5 | async-start | bytes 1572864 | tf_op jit(solution)/shard_map/all_to_all | solution.py:162
  350.5 3.5 reshape.532
  355.0 1.9 reshape.531
  356.9 15.8 %all-to-all-done.5 = bf16[64,18,256]{2,1,0:T(8,128)(2,1)} async-done(((bf16[64,18,256]{2,1,0:T(8,128)(2,1)}), bf16[64,18,256]{2,1,0:T(8,128)(2,1)}, u32[]{:S(2)}, u32[]{:S(2)}) %all-to-all-start.5) | async-done | bytes 589856 | tf_op jit(solution)/shard_map/all_to_all | solution.py:162
  372.7 1.3 reshape.534
  374.0 2.7 gather_fusion.2
  377.2 2.5 fusion.26
  (77 shorter events, 16.8 us)
Async XLA Ops:
  6.5 326.0 %copy-start = (bf16[1,1408,256]{2,1,0:T(8,128)(2,1)S(1)}, bf16[1,1408,256]{2,1,0:T(8,128)(2,1)}, u32[]{:S(2)}) copy-start(bf16[1,1408,256]{2,1,0:T(8,128)(2,1)} %param.30) | copy-start | bytes 2162692
  6.5 77.7 %all-gather.5.cloned.1.call-start = ((), (), s32[]{:S(2)}) async-start(), calls=%async_computation.6 | async-start | bytes 3907584 | tf_op jit(solution)/shard_map/all_gather | solution.py:59
  27.6 64.5 %copy-start.4 = (bf16[128,2048]{1,0:T(8,128)(2,1)S(1)}, bf16[128,2048]{1,0:T(8,128)(2,1)}, u32[]{:S(2)}) copy-start(bf16[128,2048]{1,0:T(8,128)(2,1)} %param.24) | copy-start | bytes 1572868
  89.4 14.9 %collective-permute-start = (bf16[8,4,420,128]{3,0,2,1:T(8,128)(2,1)}, bf16[8,4,420,128]{3,0,2,1:T(8,128)(2,1)}, u32[]{:S(2)}, u32[]{:S(2)}) collective-permute-start(bf16[8,4,420,128]{3,0,2,1:T(8,128)(2,1)} %copy.63), channel_id=1, source_target_pairs={{0,8},{8,0},{1,9},{9,1},{2,10},{10,2},{3,11},{11,3},{4,12},{12,4},... | collective-permute-start | bytes 10321928 | tf_op jit(solution)/shard_map/ppermute | solution.py:60
  94.7 5.1 %copy-start.1 = (s32[64]{0:T(128)S(1)}, s32[64]{0:T(128)}, u32[]{:S(2)}) copy-start(s32[64]{0:T(128)} %param.23) | copy-start | bytes 772
  94.7 54.4 %all-to-all-start.1 = ((bf16[8,128,2048]{2,1,0:T(8,128)(2,1)}), bf16[8,128,2048]{2,1,0:T(8,128)(2,1)}, u32[]{:S(2)}, u32[]{:S(2)}) async-start(bf16[8,128,2048]{2,1,0:T(8,128)(2,1)} %broadcast_in_dim.52), calls=%async_computation.1 | async-start | bytes 8388608 | tf_op jit(solution)/shard_map/all_to_all | solution.py:21
  107.8 2.8 copy-start.2
  122.8 4.2 %copy-start.6 = (bf16[128,128]{1,0:T(8,128)(2,1)S(1)}, bf16[128,128]{1,0:T(8,128)(2,1)}, u32[]{:S(2)}) copy-start(bf16[128,128]{1,0:T(8,128)(2,1)} %param.18) | copy-start | bytes 98308
  133.7 19.2 %copy-start.7 = (s32[128,6]{0,1:T(8,128)S(1)}, s32[128,6]{0,1:T(8,128)}, u32[]{:S(2)}) copy-start(s32[128,6]{0,1:T(8,128)} %param.27) | copy-start | bytes 9220
  133.7 19.6 %copy-start.8 = (bf16[2048]{0:T(1024)(128)(2,1)S(1)}, bf16[2048]{0:T(1024)(128)(2,1)}, u32[]{:S(2)}) copy-start(bf16[2048]{0:T(1024)(128)(2,1)} %param.25) | copy-start | bytes 12292
  149.1 17.1 %all-to-all-start = ((bf16[8,480,128]{2,1,0:T(8,128)(2,1)}), bf16[8,480,128]{2,1,0:T(8,128)(2,1)S(1)}, u32[]{:S(2)}, u32[]{:S(2)}) async-start(bf16[8,480,128]{2,1,0:T(8,128)(2,1)} %pad_maximum_fusion.1), calls=%async_computation | async-start | bytes 1966080 | tf_op jit(solution)/shard_map/all_to_all | solution.py:106
  172.8 36.1 %all-to-all-start.2 = ((bf16[64,18,256]{2,1,0:T(8,128)(2,1)}), bf16[64,18,256]{2,1,0:T(8,128)(2,1)}, u32[]{:S(2)}, u32[]{:S(2)}) async-start(bf16[64,18,256]{2,1,0:T(8,128)(2,1)} %reshape.528), calls=%async_computation.2 | async-start | bytes 1572864 | tf_op jit(solution)/shard_map/all_to_all | solution.py:143
  214.7 68.2 %all-to-all-start.3 = ((bf16[8,1240,256]{2,1,0:T(8,128)(2,1)}), bf16[8,1240,256]{2,1,0:T(8,128)(2,1)}, u32[]{:S(2)}, u32[]{:S(2)}) async-start(bf16[8,1240,256]{2,1,0:T(8,128)(2,1)} %broadcast_in_dim.53), calls=%async_computation.3 | async-start | bytes 10158080 | tf_op jit(solution)/shard_map/all_to_all | solution.py:21
  282.9 4.3 %copy-start.3 = (bf16[22,8,8,256]{3,2,1,0:T(8,128)(2,1)S(1)}, bf16[22,8,8,256]{3,2,1,0:T(8,128)(2,1)}, u32[]{:S(2)}) copy-start(bf16[22,8,8,256]{3,2,1,0:T(8,128)(2,1)} %copy.82) | copy-start | bytes 2162692
  332.6 16.5 %copy-start.5 = (bf16[2048,64]{0,1:T(8,128)(2,1)S(1)}, bf16[2048,64]{0,1:T(8,128)(2,1)}, u32[]{:S(2)}) copy-start(bf16[2048,64]{0,1:T(8,128)(2,1)} %param.26) | copy-start | bytes 786436
  336.6 36.1 %all-to-all-start.5 = ((bf16[64,18,256]{2,1,0:T(8,128)(2,1)}), bf16[64,18,256]{2,1,0:T(8,128)(2,1)}, u32[]{:S(2)}, u32[]{:S(2)}) async-start(bf16[64,18,256]{2,1,0:T(8,128)(2,1)} %reshape.533), calls=%async_computation.5 | async-start | bytes 1572864 | tf_op jit(solution)/shard_map/all_to_all | solution.py:162
Sparse Core Ops, SparseCore 0:
  27.7 56.4 all-gather.4

commit v4 on v2

--- a/solution.py
+++ b/solution.py
@@ -3,10 +3,10 @@
 
 import jax
 import jax.numpy as jnp
-import numpy as np
 from jax import lax
 from jax.sharding import Mesh
 from jax.sharding import PartitionSpec as P
+
 
 D = 2048
 HD = 128
@@ -15,20 +15,6 @@
 
 SEQ = ("yh", "z", "c")
 TP = ("x", "yl")
-
-
-def gather_seq(x):
-    g = lax.all_gather(x, "yh", axis=0)
-    g = lax.all_gather(g, "z", axis=0)
-    g = lax.all_gather(g, "c", axis=0)
-    return g
-
-
-def tp_blocks(x, n_tp):
-    out = [x]
-    for k in range(1, n_tp):
-        out.append(lax.ppermute(x, TP, [(j, (j + k) % n_tp) for j in range(n_tp)]))
-    return out
 
 
 def tp_gather(x, n_tp):
@@ -71,7 +57,8 @@
         [key_cache, key_new, value_cache, value_new, wpack.reshape(w_rows, HD)], 0
     )
     g = lax.all_gather(kv, "yh", axis=0)
-    g = lax.all_gather(g, "z", axis=0).reshape(n_z * n_yh, kv.shape[0], HD)
+    g = lax.all_gather(g, "z", axis=0)
+    g = g.reshape(n_z * n_yh, kv.shape[0], HD)
     other = lax.ppermute(g, "c", [(0, 1), (1, 0)])
     my_c = lax.axis_index("c")
     kv_rows = 2 * (block_rows + tok_rows)

time: 389 us -> 389 us (level)
  no operation moved by 1% of the time
where the time goes in v4:
time: 389 us; the launch traced here: 387 us
  waiting for transfers between devices  165 us (42%)
  local copies, waits for them, and re-layouts  65.4 us (17%)
  blocking collectives  58.3 us (15%)
  starting transfers between devices  43.8 us (11%)
  matrix products  28.1 us (7%)
  between operations  13.9 us (4%)
  other arithmetic  12.4 us (3%)
    all_to_all x2, waiting for transfers between devices, tp_gather(): return lax.all_to_all(b, TP, split_axis=0, concat_axis=0, tiled=True)  63.2 us
    all_gather x1, waiting for transfers between devices, local(): g = lax.all_gather(g, 'z', axis=0)  56.6 us
    all_to_all x1, blocking collectives, tp_gather(): return lax.all_to_all(b, TP, split_axis=0, concat_axis=0, tiled=True)  41.1 us
    all_to_all x1, waiting for transfers between devices, local(): recv = lax.all_to_all(buffer, SEQ, split_axis=0, concat_axis=0, tiled=True)  20.4 us
    all_gather x1, blocking collectives, local(): g = lax.all_gather(kv, 'yh', axis=0)  17.2 us
    all_to_all x1, waiting for transfers between devices, local(): returned = lax.all_to_all(out, SEQ, split_axis=0, concat_axis=0, tiled=True)  15.8 us
    all_to_all x2, starting transfers between devices, tp_gather(): return lax.all_to_all(b, TP, split_axis=0, concat_axis=0, tiled=True)  14.2 us
    unnamed x57, local copies, waits for them, and re-layouts  12.9 us
  transfers between devices with their start and end apart: 7, of which 6 were waited for; matrix products, arithmetic and copies ran while one was open for 16% of the time, Pallas kernels for 0%

profile of v4, /device:TPU:1, one launch (start us, length us, event | category | flops | bytes accessed | tf_op | source)
XLA Modules:
  0.0 387.2 jit_solution(10407411667001875815)
XLA Ops:
  10.4 17.2 %all-gather.2 = bf16[4,420,128]{2,1,0:T(8,128)(2,1)} all-gather(bf16[1,420,128]{2,1,0:T(8,128)(2,1)S(1)} %bitcast.138), channel_id=2, replica_groups=mesh['yh'=4,'z'=8,'c'=2,'x'=4,'yl'=2] {'yh'}, dimensions={0}, use_global_device_ids=true | all-gather | bytes 537600 | tf_op jit(solution)/shard_map/all_gather | solution.py:59
  27.6 56.6 %all-gather.5.cloned.1.call-done = bf16[32,420,128]{2,1,0:T(8,128)(2,1)} async-done(((bf16[4,420,128]{2,1,0:T(8,128)(2,1)}), bf16[32,420,128]{2,1,0:T(8,128)(2,1)}) %all-gather.5.cloned.1.call-update) | async-done | bytes 3440656 | tf_op jit(solution)/shard_map/all_gather | solution.py:60
  84.3 4.3 %copy.81 = bf16[32,420,128]{2,0,1:T(8,128)(2,1)} copy(bf16[32,420,128]{2,1,0:T(8,128)(2,1)} %all-gather.5.cloned.1.call-done) | data formatting | bytes 6881280 | tf_op jit(solution)/shard_map/all_gather | solution.py:60
  88.5 2.7 collective-permute-start
  91.3 2.5 broadcast_in_dim.44
  93.8 5.0 %all-to-all-start.1 = ((bf16[8,128,2048]{2,1,0:T(8,128)(2,1)}), bf16[8,128,2048]{2,1,0:T(8,128)(2,1)}, u32[]{:S(2)}, u32[]{:S(2)}) async-start(bf16[8,128,2048]{2,1,0:T(8,128)(2,1)} %broadcast_in_dim.44), calls=%async_computation.1 | async-start | bytes 8388608 | tf_op jit(solution)/shard_map/all_to_all | solution.py:22
  101.3 1.6 fusion.61
  103.0 1.4 fusion.67
  104.4 2.7 fusion.60
  107.1 3.5 fusion.68
  110.6 1.7 broadcast_select_fusion.1
  112.3 1.5 maximum_bitcast_fusion
  114.7 2.9 fusion.63
  117.6 1.4 copy.105
  121.3 5.9 %reshape.357 = bf16[64,3,32,176]{3,2,1,0:T(8,128)(2,1)} reshape(bf16[4,8,2,132,128]{4,3,2,1,0:T(8,128)(2,1)S(1)} %copy.87) | data formatting | bytes 4325376 | tf_op jit(solution)/shard_map/reshape | solution.py:69
  127.2 3.6 fusion.64
  130.8 1.5 reshape_reshape_squeeze.3
  139.6 8.6 %all-to-all-done.1 = bf16[8,128,2048]{2,1,0:T(8,128)(2,1)} async-done(((bf16[8,128,2048]{2,1,0:T(8,128)(2,1)}), bf16[8,128,2048]{2,1,0:T(8,128)(2,1)}, u32[]{:S(2)}, u32[]{:S(2)}) %all-to-all-start.1) | async-done | bytes 4194336 | tf_op jit(solution)/shard_map/all_to_all | solution.py:22
  148.2 3.7 all-to-all-start
  152.4 1.8 reduce-window.6
  156.1 9.3 %all-to-all-done = bf16[8,480,128]{2,1,0:T(8,128)(2,1)S(1)} async-done(((bf16[8,480,128]{2,1,0:T(8,128)(2,1)}), bf16[8,480,128]{2,1,0:T(8,128)(2,1)S(1)}, u32[]{:S(2)}, u32[]{:S(2)}) %all-to-all-start) | async-done | bytes 983072 | tf_op jit(solution)/shard_map/all_to_all | solution.py:110
  165.4 3.1 multiply_reduce_fusion.1
  168.7 1.1 convolution_convert_fusion
  169.8 2.1 reshape.359
  171.9 11.9 %all-to-all-start.2 = ((bf16[64,18,256]{2,1,0:T(8,128)(2,1)}), bf16[64,18,256]{2,1,0:T(8,128)(2,1)}, u32[]{:S(2)}, u32[]{:S(2)}) async-start(bf16[64,18,256]{2,1,0:T(8,128)(2,1)} %reshape.359), calls=%async_computation.2 | async-start | bytes 1572864 | tf_op jit(solution)/shard_map/all_to_all | solution.py:147
  183.8 1.7 fusion.69
  185.5 1.7 fusion.30
  187.6 20.4 %all-to-all-done.2 = bf16[64,18,256]{2,1,0:T(8,128)(2,1)} async-done(((bf16[64,18,256]{2,1,0:T(8,128)(2,1)}), bf16[64,18,256]{2,1,0:T(8,128)(2,1)}, u32[]{:S(2)}, u32[]{:S(2)}) %all-to-all-start.2) | async-done | bytes 589856 | tf_op jit(solution)/shard_map/all_to_all | solution.py:147
  208.0 2.1 reshape.360
  210.1 1.1 pad_maximum_fusion.1
  211.2 2.6 broadcast_in_dim.45
  213.8 9.2 %all-to-all-start.3 = ((bf16[8,1240,256]{2,1,0:T(8,128)(2,1)}), bf16[8,1240,256]{2,1,0:T(8,128)(2,1)}, u32[]{:S(2)}, u32[]{:S(2)}) async-start(bf16[8,1240,256]{2,1,0:T(8,128)(2,1)} %broadcast_in_dim.45), calls=%async_computation.3 | async-start | bytes 10158080 | tf_op jit(solution)/shard_map/all_to_all | solution.py:22
  223.0 2.2 copy.107
  225.1 2.2 copy.108
  227.3 54.7 %all-to-all-done.3 = bf16[8,1240,256]{2,1,0:T(8,128)(2,1)} async-done(((bf16[8,1240,256]{2,1,0:T(8,128)(2,1)}), bf16[8,1240,256]{2,1,0:T(8,128)(2,1)}, u32[]{:S(2)}, u32[]{:S(2)}) %all-to-all-start.3) | async-done | bytes 5079072 | tf_op jit(solution)/shard_map/all_to_all | solution.py:22
  281.9 4.3 %fusion.10 = f32[1152,176]{0,1:T(8,128)S(1)} fusion(bf16[8,1240,256]{2,1,0:T(8,128)(2,1)} %all-to-all-done.3, bf16[8,256,176]{1,0,2:T(8,128)(2,1)} %bitcast.133), kind=kOutput, calls=%fused_computation.18 | convolution fusion | flops 830472192 | bytes 6250496 | tf_op jit(solution)/shard_map/tsc,tcf->sf/dot_general | solution.py:159
  286.2 4.0 %fusion.19 = bf16[1152,176]{0,1:T(8,128)(2,1)S(1)} fusion(bf16[8,1240,256]{2,1,0:T(8,128)(2,1)} %all-to-all-done.3, f32[1152,176]{0,1:T(8,128)S(1)} %fusion.10, bf16[8,256,176]{1,0,2:T(8,128)(2,1)S(1)} %bitcast.132), kind=kOutput, calls=%fused_computation.21 | convolution fusion | flops 831688704 | bytes 6656000 | tf_op jit(solution)/shard_map/tsc,tcf->sf/dot_general | solution.py:160
  290.5 41.1 %all_to_all.30 = bf16[8,1152,176]{1,2,0:T(8,128)(2,1)S(1)} all-to-all(bf16[8,1152,176]{1,2,0:T(8,128)(2,1)S(1)} %broadcast_in_dim.46), channel_id=1, replica_groups=mesh['yh'=4,'z'=8,'c'=2,'x'=4,'yl'=2] {'x','yl'}, dimensions={0} | all-to-all | bytes 6488064 | tf_op jit(solution)/shard_map/all_to_all | solution.py:22
  331.6 2.0 fusion.9
  333.6 2.1 reshape.364
  335.6 11.2 %all-to-all-start.5 = ((bf16[64,18,256]{2,1,0:T(8,128)(2,1)}), bf16[64,18,256]{2,1,0:T(8,128)(2,1)}, u32[]{:S(2)}, u32[]{:S(2)}) async-start(bf16[64,18,256]{2,1,0:T(8,128)(2,1)} %reshape.364), calls=%async_computation.5 | async-start | bytes 1572864 | tf_op jit(solution)/shard_map/all_to_all | solution.py:166
  348.8 3.5 reshape.363
  353.8 1.9 reshape.362
  355.7 15.8 %all-to-all-done.5 = bf16[64,18,256]{2,1,0:T(8,128)(2,1)} async-done(((bf16[64,18,256]{2,1,0:T(8,128)(2,1)}), bf16[64,18,256]{2,1,0:T(8,128)(2,1)}, u32[]{:S(2)}, u32[]{:S(2)}) %all-to-all-start.5) | async-done | bytes 589856 | tf_op jit(solution)/shard_map/all_to_all | solution.py:166
  371.5 1.3 reshape.365
  372.8 2.7 gather_fusion.2
  376.6 1.6 multiply_reduce_fusion
  378.2 2.2 fusion.29
  (116 shorter events, 24.2 us)
Async XLA Ops:
  6.5 325.1 %copy-start = (bf16[1,1408,256]{2,1,0:T(8,128)(2,1)S(1)}, bf16[1,1408,256]{2,1,0:T(8,128)(2,1)}, u32[]{:S(2)}) copy-start(bf16[1,1408,256]{2,1,0:T(8,128)(2,1)} %param.30) | copy-start | bytes 2162692
  6.5 77.7 %all-gather.5.cloned.1.call-start = ((), (), s32[]{:S(2)}) async-start(), calls=%async_computation.6 | async-start | bytes 3907584 | tf_op jit(solution)/shard_map/all_gather | solution.py:60
  27.6 63.7 %copy-start.9 = (bf16[128,2048]{1,0:T(8,128)(2,1)S(1)}, bf16[128,2048]{1,0:T(8,128)(2,1)}, u32[]{:S(2)}) copy-start(bf16[128,2048]{1,0:T(8,128)(2,1)} %param.24) | copy-start | bytes 1572868
  88.5 22.1 %collective-permute-start = (bf16[32,420,128]{2,0,1:T(8,128)(2,1)}, bf16[32,420,128]{2,0,1:T(8,128)(2,1)}, u32[]{:S(2)}, u32[]{:S(2)}) collective-permute-start(bf16[32,420,128]{2,0,1:T(8,128)(2,1)} %copy.81), channel_id=1, source_target_pairs={{0,8},{8,0},{1,9},{9,1},{2,10},{10,2},{3,11},{11,3},{4,12},{12,4},... | collective-permute-start | bytes 10321928 | tf_op jit(solution)/shard_map/ppermute | solution.py:62
  93.8 5.1 %copy-start.1 = (s32[64]{0:T(128)S(1)}, s32[64]{0:T(128)}, u32[]{:S(2)}) copy-start(s32[64]{0:T(128)} %param.23) | copy-start | bytes 772
  93.8 9.1 %copy-start.14 = (bf16[128,128]{1,0:T(8,128)(2,1)S(1)}, bf16[128,128]{1,0:T(8,128)(2,1)}, u32[]{:S(2)}) copy-start(bf16[128,128]{1,0:T(8,128)(2,1)} %param.18) | copy-start | bytes 98308
  93.8 54.4 %all-to-all-start.1 = ((bf16[8,128,2048]{2,1,0:T(8,128)(2,1)}), bf16[8,128,2048]{2,1,0:T(8,128)(2,1)}, u32[]{:S(2)}, u32[]{:S(2)}) async-start(bf16[8,128,2048]{2,1,0:T(8,128)(2,1)} %broadcast_in_dim.44), calls=%async_computation.1 | async-start | bytes 8388608 | tf_op jit(solution)/shard_map/all_to_all | solution.py:22
  101.2 5.9 %copy-start.21 = (s32[128]{0:T(128)}, s32[128]{0:T(128)S(1)}, u32[]{:S(2)}) copy-start(s32[128]{0:T(128)S(1)} %iota_add_fusion) | copy-start | bytes 1540
  130.8 1.5 copy-start.3
  132.3 0.9 copy-start.10
  132.3 0.9 copy-start.15
  132.3 0.9 copy-start.18
  132.3 1.1 copy-start.22
  132.7 1.6 copy-start.19
  132.7 1.6 copy-start.20
  132.8 1.6 copy-start.6
  133.2 1.6 copy-start.4
  134.8 0.9 copy-start.13
  134.8 1.3 copy-start.5
  136.1 1.2 copy-start.7
  137.3 0.9 copy-start.12
  138.5 13.5 %copy-start.16 = (s32[128,6]{0,1:T(8,128)S(1)}, s32[128,6]{0,1:T(8,128)}, u32[]{:S(2)}) copy-start(s32[128,6]{0,1:T(8,128)} %param.27) | copy-start | bytes 9220
  138.5 13.8 %copy-start.17 = (bf16[2048]{0:T(1024)(128)(2,1)S(1)}, bf16[2048]{0:T(1024)(128)(2,1)}, u32[]{:S(2)}) copy-start(bf16[2048]{0:T(1024)(128)(2,1)} %param.25) | copy-start | bytes 12292
  148.2 17.1 %all-to-all-start = ((bf16[8,480,128]{2,1,0:T(8,128)(2,1)}), bf16[8,480,128]{2,1,0:T(8,128)(2,1)S(1)}, u32[]{:S(2)}, u32[]{:S(2)}) async-start(bf16[8,480,128]{2,1,0:T(8,128)(2,1)} %pad_maximum_fusion), calls=%async_computation | async-start | bytes 1966080 | tf_op jit(solution)/shard_map/all_to_all | solution.py:110
  171.9 36.1 %all-to-all-start.2 = ((bf16[64,18,256]{2,1,0:T(8,128)(2,1)}), bf16[64,18,256]{2,1,0:T(8,128)(2,1)}, u32[]{:S(2)}, u32[]{:S(2)}) async-start(bf16[64,18,256]{2,1,0:T(8,128)(2,1)} %reshape.359), calls=%async_computation.2 | async-start | bytes 1572864 | tf_op jit(solution)/shard_map/all_to_all | solution.py:147
  213.8 68.2 %all-to-all-start.3 = ((bf16[8,1240,256]{2,1,0:T(8,128)(2,1)}), bf16[8,1240,256]{2,1,0:T(8,128)(2,1)}, u32[]{:S(2)}, u32[]{:S(2)}) async-start(bf16[8,1240,256]{2,1,0:T(8,128)(2,1)} %broadcast_in_dim.45), calls=%async_computation.3 | async-start | bytes 10158080 | tf_op jit(solution)/shard_map/all_to_all | solution.py:22
  281.9 4.3 %copy-start.8 = (bf16[22,8,8,256]{3,2,1,0:T(8,128)(2,1)S(1)}, bf16[22,8,8,256]{3,2,1,0:T(8,128)(2,1)}, u32[]{:S(2)}) copy-start(bf16[22,8,8,256]{3,2,1,0:T(8,128)(2,1)} %copy.108) | copy-start | bytes 2162692
  335.6 16.6 %copy-start.11 = (bf16[2048,64]{0,1:T(8,128)(2,1)S(1)}, bf16[2048,64]{0,1:T(8,128)(2,1)}, u32[]{:S(2)}) copy-start(bf16[2048,64]{0,1:T(8,128)(2,1)} %param.26) | copy-start | bytes 786436
  335.6 35.8 %all-to-all-start.5 = ((bf16[64,18,256]{2,1,0:T(8,128)(2,1)}), bf16[64,18,256]{2,1,0:T(8,128)(2,1)}, u32[]{:S(2)}, u32[]{:S(2)}) async-start(bf16[64,18,256]{2,1,0:T(8,128)(2,1)} %reshape.364), calls=%async_computation.5 | async-start | bytes 1572864 | tf_op jit(solution)/shard_map/all_to_all | solution.py:166
  375.5 2.7 copy-start.2
Sparse Core Ops, SparseCore 0:
  27.7 56.4 all-gather.4
